TPU v7x, 256 devices: a whole 4x4x8 slice. The times are simulated.
256 devices in a mesh: grp: 8 (over y, z_hi), tp: 4 (over z_lo), ffn: 8 (over x, core).
Axes of the slice: x: 4, y: 4, z: 8 (z_hi: 2, z_lo: 4; z = z_hi * 4 + z_lo), core: 2. Of those that a mesh axis runs over, the one named last changes fastest.
Arguments:
- queries: bfloat16 [768, 8192], P('grp', 'tp'), may hold values from -320 to 320
- new_kv: bfloat16 [2, 768, 1024], P(None, 'grp', 'tp'), may hold values from -12 to 12
- kv_cache: bfloat16 [2, 8, 16384, 1024], P(None, 'grp', 'ffn', 'tp'), may hold values from -12 to 12
- lengths: int32 [8], P('grp'), may hold values from 1 to 96, as said below
- prefixes: int32 [8], P('grp'), may hold values from 0 to 16384, as said below
- resid: bfloat16 [768, 8192], P('grp', 'ffn'), may hold values from -0.29882812 to 0.29882812
- out_weight: bfloat16 [8192, 8192], P('tp', 'ffn'), may hold values from -0.0625 to 0.0625
- gain: bfloat16 [8192], P('ffn'), may hold values from 0.099609375 to 1.8984375
- gate_weight: bfloat16 [8192, 29568], P('ffn', ('grp', 'tp')), may hold values from -0.0625 to 0.0625
- up_weight: bfloat16 [8192, 29568], P('ffn', ('grp', 'tp')), may hold values from -0.0625 to 0.0625
- down_weight: bfloat16 [29568, 8192], P(('grp', 'tp'), 'ffn'), may hold values from -0.03125 to 0.03125
Outputs:
- layer_out: bfloat16 [768, 8192], P(('grp', 'tp'), 'ffn')
Inputs may be any that keep to these rules, and one draw needn't show every extreme that they name: `lengths`: some group has a full block of 96 live slots. `prefixes`: some group has all 16384 cached positions in use.
All inputs are finite; a program needn't handle non-finite values.
Results may differ from a plain program's by a relative error of at most 0.02.
Values may be sent and summed in bfloat16 or wider, within the bound.
A program may use at most 64 MiB of HBM per device.

v0:
```python
import math

import jax
import jax.numpy as jnp
from jax import lax
from jax.sharding import PartitionSpec as P

D = 8192
DH = 128


negative = -1e30


def merged(x, axis, combine):
    everything = jax.tree.map(lambda part: lax.all_gather(part, axis), x)
    leading = jax.tree.map(lambda part: part[0], everything)

    def hop(k, so_far):
        return combine(so_far, jax.tree.map(lambda part: part[k], everything))

    return lax.fori_loop(1, lax.axis_size(axis), hop, leading)


def combine_parts(first, second):
    top = jnp.maximum(first[0], second[0])
    left = jnp.exp(first[0] - top)
    right = jnp.exp(second[0] - top)
    total = first[1] * left + second[1] * right
    values = first[2] * left[..., None] + second[2] * right[..., None]
    return (top, total, values)


def body(
    queries,
    new_kv,
    kv_cache,
    lengths,
    prefixes,
    resid,
    out_weight,
    gain,
    gate_weight,
    up_weight,
    down_weight,
):
    span, qcols = queries.shape
    kcols = new_kv.shape[2]
    local_kv = kcols // DH
    group = qcols // DH // local_kv
    cache_len = kv_cache.shape[2]
    length = lengths[0]
    prefix = prefixes[0]
    width_index = lax.axis_index("ffn")
    shard_start = width_index * cache_len
    query_heads = (
        queries.reshape(span, local_kv, group, DH)
        .transpose(1, 2, 0, 3)
        .reshape(local_kv, group * span, DH)
    )
    row_pos = jnp.tile(jnp.arange(span, dtype=jnp.int32), group)
    inv_scale = 1.0 / math.sqrt(DH)

    def update(state, keys, values, valid):
        top, total, acc = state
        scores = (
            jnp.einsum("hrd,hkd->hrk", query_heads, keys, preferred_element_type=jnp.float32)
            * inv_scale
        )
        scores = jnp.where(valid[None], scores, negative)
        new_top = jnp.maximum(top, jnp.max(scores, axis=-1))
        probs = jnp.where(valid[None], jnp.exp(scores - new_top[..., None]), 0.0)
        factor = jnp.exp(top - new_top)
        total = total * factor + jnp.sum(probs, axis=-1)
        acc = acc * factor[..., None] + jnp.einsum(
            "hrk,hkd->hrd", probs, values.astype(jnp.float32)
        )
        return (new_top, total, acc)

    block = math.gcd(512, cache_len)
    blocks = cache_len // block
    cache_keys = kv_cache[0, 0].reshape(blocks, block, local_kv, DH).transpose(0, 2, 1, 3)
    cache_values = kv_cache[1, 0].reshape(blocks, block, local_kv, DH).transpose(0, 2, 1, 3)
    rows = group * span
    start_state = (
        jnp.full((local_kv, rows), negative, jnp.float32),
        jnp.zeros((local_kv, rows), jnp.float32),
        jnp.zeros((local_kv, rows, DH), jnp.float32),
    )

    def cache_step(state, items):
        keys, values, index = items
        positions = shard_start + index * block + jnp.arange(block, dtype=jnp.int32)
        valid = jnp.broadcast_to((positions < prefix)[None, :], (rows, block))
        return (update(state, keys, values, valid), None)

    state, unused = lax.scan(
        cache_step, start_state, (cache_keys, cache_values, jnp.arange(blocks, dtype=jnp.int32))
    )
    block_keys = new_kv[0].reshape(span, local_kv, DH).transpose(1, 0, 2)
    block_values = new_kv[1].reshape(span, local_kv, DH).transpose(1, 0, 2)
    slots = jnp.arange(span, dtype=jnp.int32)[None, :]
    new_valid = (slots < length) & (slots <= row_pos[:, None]) & (width_index == 0)
    state = update(state, block_keys, block_values, new_valid)
    top, total, acc = merged(state, "ffn", combine_parts)
    heads = acc / total[..., None]
    attn = (
        heads.reshape(local_kv, group, span, DH)
        .transpose(2, 0, 1, 3)
        .reshape(span, qcols)
        .astype(jnp.bfloat16)
    )
    partial_value = jnp.dot(attn, out_weight, preferred_element_type=jnp.float32)
    summed = lax.psum(partial_value, "tp")
    h1 = (summed + resid.astype(jnp.float32)).astype(jnp.bfloat16)
    all_rows = lax.all_gather(h1, "grp", axis=0, tiled=True)
    rows_f = all_rows.astype(jnp.float32)
    squares = jnp.sum(rows_f * rows_f, axis=1)
    scaled = (rows_f * gain.astype(jnp.float32)[None, :]).astype(jnp.bfloat16)
    gate = jnp.dot(scaled, gate_weight, preferred_element_type=jnp.float32)
    upper = jnp.dot(scaled, up_weight, preferred_element_type=jnp.float32)
    rows_here = span // lax.axis_size("tp")
    gate, upper, squares = lax.psum((gate, upper, squares), "ffn")
    inv_rms = lax.rsqrt(squares / D + 1e-06)
    hidden = (jax.nn.silu(gate * inv_rms[:, None]) * (upper * inv_rms[:, None])).astype(
        jnp.bfloat16
    )
    down_rows = lax.psum_scatter(
        jnp.dot(hidden, down_weight, preferred_element_type=jnp.float32),
        ("grp", "tp"),
        scatter_dimension=0,
        tiled=True,
    )
    row_start = lax.axis_index("tp") * rows_here
    own = lax.dynamic_slice_in_dim(h1, row_start, rows_here, 0)
    live = row_start + jnp.arange(rows_here, dtype=jnp.int32) < length
    return jnp.where(live[:, None], own.astype(jnp.float32) + down_rows, 0.0).astype(jnp.bfloat16)


def solution(mesh):
    return jax.shard_map(
        body,
        mesh=mesh,
        in_specs=(
            P("grp", "tp"),
            P(None, "grp", "tp"),
            P(None, "grp", "ffn", "tp"),
            P("grp"),
            P("grp"),
            P("grp", "ffn"),
            P("tp", "ffn"),
            P("ffn"),
            P("ffn", ("grp", "tp")),
            P("ffn", ("grp", "tp")),
            P(("grp", "tp"), "ffn"),
        ),
        out_specs=P(("grp", "tp"), "ffn"),
        check_vma=False,
    )
```

profile of v0, /device:TPU:2, one launch (start us, length us, event | category | flops | bytes accessed | tf_op | source)
XLA Modules:
  0.0 559.2 jit_solution(7451356754690004521)
XLA Ops:
  9.5 3.0 fusion.47
  12.5 1.3 reshape_squeeze.13
  13.9 2.1 reshape_squeeze.12
  16.0 28.8 %while.35 = (s32[]{:T(128)}, f32[2,768]{1,0:T(2,128)S(1)}, f32[2,768]{1,0:T(2,128)S(1)}, f32[2,768,128]{2,1,0:T(8,128)}, s32[4]{0:T(128)S(1)}, /*index=5*/s32[]{...) while((s32[]{:T(128)}, f32[2,768]{1,0:T(2,128)S(1)}, ...), condition=%wide.region_3.4_spmd.clone, body=%wide.region_0.3_spmd.clone.sunk | while | flops 412688896 | bytes 19368184 | solution.py:97
  20.8 1.5 fusion.71
  25.1 1.3 constant_dynamic-slice_fusion.3
  28.0 1.5 fusion.71
  35.2 1.5 fusion.71
  42.4 1.5 fusion.71
  45.4 2.5 convolution_add_fusion
  48.0 12.9 %all-gather.4 = f32[8,2,768]{2,1,0:T(2,128)S(1)} all-gather(f32[1,2,768]{2,1,0:T(2,128)S(1)} %get-tuple-element.336), channel_id=3, replica_groups=mesh['grp'=8,'tp'=4,'ffn'=8] {'ffn'}, dimensions={0}, use_global_device_ids=true | all-gather | bytes 55296 | tf_op jit(solution)/shard_map/all_gather | solution.py:16
  60.8 12.8 %all-gather.3 = f32[8,2,768]{2,1,0:T(2,128)S(1)} all-gather(f32[1,2,768]{2,1,0:T(2,128)S(1)} %bitcast.107), channel_id=2, replica_groups=mesh['grp'=8,'tp'=4,'ffn'=8] {'ffn'}, dimensions={0}, use_global_device_ids=true | all-gather | bytes 55296 | tf_op jit(solution)/shard_map/all_gather | solution.py:16
  73.6 20.0 %all-gather.10.cloned.1.call-done = f32[16,768,128]{2,1,0:T(8,128)} async-done(((f32[2,768,128]{2,1,0:T(8,128)}), f32[16,768,128]{2,1,0:T(8,128)}) %all-gather.10.cloned.1.call-update) | async-done | bytes 6291472 | tf_op jit(solution)/shard_map/all_gather | solution.py:16
  94.8 13.0 %while.34 = (s32[]{:T(128)}, f32[2,768]{1,0:T(2,128)S(1)}, f32[2,768]{1,0:T(2,128)S(1)}, f32[2,768,128]{2,1,0:T(8,128)S(1)}, f32[8,2,768]{2,1,0:T(2,128)S(1)}, /...) while((s32[]{:T(128)}, f32[2,768]{1,0:T(2,128)S(1)}, ...), condition=%wide.region_7.8_spmd, body=%wide.region_6.7_spmd.sunk | while | flops 599045 | bytes 2420879 | solution.py:22
  94.9 1.8 fusion.65
  96.7 1.8 fusion.65
  98.6 1.8 fusion.65
  100.5 1.8 fusion.65
  102.3 1.8 fusion.65
  104.2 1.8 fusion.65
  106.0 1.8 fusion.65
  108.3 3.8 fusion.32
  112.2 52.0 %all-reduce.4.cloned.1.call-done = f32[96,1024]{1,0:T(8,128)} async-done(((f32[96,1024]{1,0:T(8,128)}), f32[96,1024]{1,0:T(8,128)}) %all-reduce.4.cloned.1.call-update) | async-done | bytes 393232 | tf_op jit(solution)/shard_map/psum | solution.py:114
  164.2 1.7 add_convert_fusion
  165.9 69.0 %all-gather.8.cloned.1.call-done = bf16[768,1024]{1,0:T(8,128)(2,1)} async-done(((bf16[96,1024]{1,0:T(8,128)(2,1)}), bf16[768,1024]{1,0:T(8,128)(2,1)}) %all-gather.8.cloned.1.call-update) | async-done | bytes 1572880 | tf_op jit(solution)/shard_map/all_gather | solution.py:116
  235.0 5.4 fusion.26
  240.4 3.3 fusion.28
  244.1 10.0 %psum.30 = f32[768]{0:T(1024)S(1)} all-reduce(f32[768]{0:T(1024)S(1)} %fusion.24), channel_id=1, replica_groups=mesh['grp'=8,'tp'=4,'ffn'=8] {'ffn'}, use_global_device_ids=true, to_apply=%region_11.12 | all-reduce | flops 768 | bytes 6144 | tf_op jit(solution)/shard_map/psum | solution.py:123
  254.2 68.5 %all-reduce.6.cloned.1.call-done = (f32[768,924]{0,1:T(8,128)}, f32[768,924]{0,1:T(8,128)}) async-done(((f32[768,924]{0,1:T(8,128)}, f32[768,924]{0,1:T(8,128)}), (f32[768,924]{0,1:T(8,128)}, f32[768,924]{0,1:T(8,128)})) %all-reduce.6.cloned.1.call-update) | async-done | bytes 5677072 | tf_op jit(solution)/shard_map/psum | solution.py:123
  322.7 6.2 %fusion.25 = f32[768,1024]{1,0:T(8,128)} fusion(bf16[924,1024]{1,0:T(8,128)(2,1)S(1)} %copy-done, f32[768,924]{0,1:T(8,128)} %get-tuple-element.328, f32[768,924]{0,1:T(8,128)} %get-tuple-element.329, f32[768]{0:T(1024)S(1)} %add_rsqrt_fusion), kind=kOutput, calls=%fused_computation.42 | convolution fusion | flops 1459003392 | bytes 10718208 | tf_op jit(solution)/shard_map/dot_general | solution.py:129
  329.0 222.1 %reduce-scatter.2.cloned.1.call-done = f32[24,1024]{1,0:T(8,128)} async-done(((f32[768,1024]{1,0:T(8,128)}), f32[24,1024]{1,0:T(8,128)}) %reduce-scatter.2.cloned.1.call-update) | async-done | bytes 98320 | tf_op jit(solution)/shard_map/reduce_scatter | solution.py:128
  551.1 1.6 select_convert_fusion
  (100 shorter events, 23.9 us)
Async XLA Ops:
  6.5 316.1 %copy-start = (bf16[924,1024]{1,0:T(8,128)(2,1)S(1)}, bf16[924,1024]{1,0:T(8,128)(2,1)}, u32[]{:S(2)}) copy-start(bf16[924,1024]{1,0:T(8,128)(2,1)} %param.25) | copy-start | bytes 5677060
  6.5 87.1 %all-gather.10.cloned.1.call-start = ((), (), s32[]{:S(2)}) async-start(), calls=%async_computation.4 | async-start | bytes 7077888 | tf_op jit(solution)/shard_map/all_gather | solution.py:16
  19.3 1.5 copy-start.2
  22.3 0.9 copy-start.3
  26.5 1.5 copy-start.2
  29.5 0.9 copy-start.3
  33.7 1.5 copy-start.2
  36.7 0.9 copy-start.3
  40.9 1.5 copy-start.2
  43.9 0.9 copy-start.3
  47.9 116.2 %all-reduce.4.cloned.1.call-start = ((), (), s32[]{:S(2)}) async-start(), calls=%async_computation.1 | async-start | bytes 786432 | tf_op jit(solution)/shard_map/psum | solution.py:114
  108.3 55.9 %copy-start.4 = (bf16[96,1024]{1,0:T(8,128)(2,1)S(1)}, bf16[96,1024]{1,0:T(8,128)(2,1)}, u32[]{:S(2)}) copy-start(bf16[96,1024]{1,0:T(8,128)(2,1)} %param.20) | copy-start | bytes 589828
  108.3 57.6 %copy-start.5 = (bf16[1024]{0:T(1024)(128)(2,1)S(1)}, bf16[1024]{0:T(1024)(128)(2,1)}, u32[]{:S(2)}) copy-start(bf16[1024]{0:T(1024)(128)(2,1)} %param.22) | copy-start | bytes 6148
  112.1 122.8 %all-gather.8.cloned.1.call-start = ((), (), s32[]{:S(2)}) async-start(), calls=%async_computation.2 | async-start | bytes 1769472 | tf_op jit(solution)/shard_map/all_gather | solution.py:116
  165.9 156.8 %all-reduce.6.cloned.1.call-start = ((), (), s32[]{:S(2)}) async-start(), calls=%async_computation.5 | async-start | bytes 11403264 | tf_op jit(solution)/shard_map/psum | solution.py:123
  235.0 5.4 copy-start.1
  235.0 5.4 copy-start.6
  243.7 307.4 %reduce-scatter.2.cloned.1.call-start = ((), (), s32[]{:S(2)}) async-start(), calls=%async_computation.3 | async-start | bytes 3244032 | tf_op jit(solution)/shard_map/reduce_scatter | solution.py:128
Sparse Core Ops, SparseCore 0:
  48.0 45.5 all-gather.9
  112.2 51.8 all-reduce.3
  167.1 67.8 all-gather.7
  243.8 78.8 all-reduce.5
  329.1 221.9 reduce-scatter.1
where the time goes:
time: 560 us; the launch traced here: 559 us
  waiting for transfers between devices  432 us (77%)
  blocking collectives  35.7 us (6%)
  matrix products  30 us (5%)
  other arithmetic  23.3 us (4%)
  local copies, waits for them, and re-layouts  21.3 us (4%)
  between operations  14.1 us (3%)
    reduce_scatter x1, waiting for transfers between devices, body(): lax.psum_scatter(jnp.dot(hidden, down_weight, preferred_element_type=jnp....  222 us
    all_gather x1, waiting for transfers between devices, body(): all_rows = lax.all_gather(h1, 'grp', axis=0, tiled=True)  69 us
    psum x1, waiting for transfers between devices, body(): gate, upper, squares = lax.psum((gate, upper, squares), 'ffn')  68.5 us
    psum x1, waiting for transfers between devices, body(): summed = lax.psum(partial_value, 'tp')  52 us
    all_gather x2, blocking collectives, merged(): everything = jax.tree.map(lambda part: lax.all_gather(part, axis), x)  25.6 us
    all_gather x1, waiting for transfers between devices, merged(): everything = jax.tree.map(lambda part: lax.all_gather(part, axis), x)  20 us
    add x7, other arithmetic, combine_parts(): values = first[2] * left[..., None] + second[2] * right[..., None]  12.6 us
  transfers between devices with their start and end apart: 5, of which 5 were waited for; matrix products, arithmetic and copies ran while one was open for 0% of the time, Pallas kernels for 0%

commit v1 on v0

v1 whole, which is shorter than its diff:
```python
import functools
import math

import jax
import jax.numpy as jnp
from jax import lax
from jax.experimental import pallas as pl
from jax.experimental.pallas import tpu as pltpu
from jax.sharding import PartitionSpec as P

MESH = pl.DeviceIdType.MESH
F32 = jnp.float32
BF16 = jnp.bfloat16

D = 8192
DH = 128
SPAN = 96
ROWS_OUT = 24
KEYS = 2048
WIDTH = 1024
HID = 924
NEG = -1e30
SCALE = math.log2(math.e) / math.sqrt(DH)


class Place:
    def __init__(self):
        g = lax.axis_index("grp")
        self.t = lax.axis_index("tp")
        self.f = lax.axis_index("ffn")
        self.y, self.zh = g // 2, g % 2
        self.x, self.c = self.f // 2, self.f % 2
        self.z = self.zh * 4 + self.t
        self.xa, self.xb = flip(self.x), 3 - self.x
        self.ya, self.yb = flip(self.y), 3 - self.y

    def ffn(self, f):
        return {"ffn": f}

    def tp(self, t):
        return {"tp": t}

    def core(self):
        return {"ffn": self.x * 2 + 1 - self.c}

    def at_x(self, x):
        return {"ffn": x * 2 + self.c}

    def at_y(self, y):
        return {"grp": y * 2 + self.zh}

    def at_z(self, step):
        z = (self.z + step + 8) % 8
        return {"grp": self.y * 2 + z // 4, "tp": z % 4}


def flip(v):
    return v + 1 - 2 * (v % 2)


class Links:
    def __init__(self, send_sems, recv_sems):
        self.send_sems, self.recv_sems = send_sems, recv_sems
        self.started = []

    def start(self, src, dst, device):
        k = len(self.started)
        copy = pltpu.make_async_remote_copy(
            src_ref=src,
            dst_ref=dst,
            send_sem=self.send_sems.at[k],
            recv_sem=self.recv_sems.at[k],
            device_id=device,
            device_id_type=MESH,
        )
        copy.start()
        self.started.append(copy)
        return copy

    def finish(self):
        for copy in self.started:
            copy.wait_send()


def greet(devices):
    barrier = pltpu.get_barrier_semaphore()
    for device in devices:
        pl.semaphore_signal(barrier, inc=1, device_id=device, device_id_type=MESH)


def greeted(devices):
    pl.semaphore_wait(pltpu.get_barrier_semaphore(), len(devices))


def in_turn(*flows):
    alive = list(flows)
    while alive:
        for flow in list(alive):
            try:
                next(flow)
            except StopIteration:
                alive.remove(flow)


def arrived(*copies):
    for copy in copies:
        copy.wait_recv()


def attention_kernel(
    length_ref, prefix_ref, q_ref, new_ref, resid_ref, cache_hbm, wo_hbm,
    h_ref,
    kv, wo, o_out, st_out, o_in, st_in, att, part_f, part_b, part_in,
    local_sems, send_sems, recv_sems,
):
    me = Place()
    links = Links(send_sems, recv_sems)
    f, t, y, z = me.f, me.t, me.y, me.z
    load_k = pltpu.make_async_copy(cache_hbm.at[0, 0], kv.at[0], local_sems.at[0])
    load_v = pltpu.make_async_copy(cache_hbm.at[1, 0], kv.at[1], local_sems.at[1])
    load_wo = pltpu.make_async_copy(wo_hbm, wo, local_sems.at[2])
    load_k.start()
    load_v.start()
    load_wo.start()
    friends = [me.ffn((f + d) % 8) for d in range(1, 8)]
    friends += [me.tp((t + d) % 4) for d in range(1, 4)]
    friends += [me.at_y(me.ya), me.at_y(me.yb), me.at_z(1), me.at_z(-1)]
    greet(friends)

    length, prefix = length_ref[0], prefix_ref[0]
    lanes = lax.broadcasted_iota(jnp.int32, (1, KEYS), 1)
    bias = jnp.where(f * KEYS + lanes < prefix, 0.0, NEG).astype(F32)
    slot = lax.broadcasted_iota(jnp.int32, (SPAN, SPAN), 0)
    key = lax.broadcasted_iota(jnp.int32, (SPAN, SPAN), 1)
    limit = jnp.where(f == 0, length, 0)
    new_bias = jnp.where((key <= slot) & (key < limit), 0.0, NEG).astype(F32)
    new_bias = jnp.concatenate([new_bias] * 4, axis=0)
    lane = lax.broadcasted_iota(jnp.int32, (4 * SPAN, 128), 1)
    load_k.wait()
    load_v.wait()

    def attend(step, carry):
        half, h = step // 2, step % 2
        cols = pl.ds(pl.multiple_of(h * DH, DH), DH)
        keys, values = kv[0, :, cols], kv[1, :, cols]
        new_keys, new_values = new_ref[0, :, cols], new_ref[1, :, cols]
        q = jnp.concatenate(
            [
                q_ref[:, pl.ds(pl.multiple_of((h * 8 + half * 4 + i) * DH, DH), DH)]
                for i in range(4)
            ],
            axis=0,
        )
        nt = (((1,), (1,)), ((), ()))
        s = lax.dot_general(q, keys, nt, preferred_element_type=F32) + bias
        s_new = lax.dot_general(q, new_keys, nt, preferred_element_type=F32) + new_bias
        top = jnp.maximum(
            jnp.max(s, axis=1, keepdims=True), jnp.max(s_new, axis=1, keepdims=True)
        )
        p = jnp.exp2((s - top) * SCALE).astype(BF16)
        p_new = jnp.exp2((s_new - top) * SCALE).astype(BF16)
        wide = jnp.concatenate([values, jnp.ones((KEYS, DH), BF16)], axis=1)
        wide_new = jnp.concatenate([new_values, jnp.ones((SPAN, DH), BF16)], axis=1)
        acc = jnp.dot(p, wide, preferred_element_type=F32) + jnp.dot(
            p_new, wide_new, preferred_element_type=F32
        )
        total = acc[:, DH:]
        out = (acc[:, :DH] / total).astype(BF16)
        stats = jnp.where(lane == 0, top, jnp.where(lane == 1, total, 0.0))
        for i in range(4):
            rows = slice(i * SPAN, (i + 1) * SPAN)
            o_out[half * 4 + i, h] = out[rows]
            square = jnp.concatenate([stats[rows], jnp.zeros((32, 128), F32)], axis=0)
            st_out[half * 4 + i, h] = jnp.transpose(square)[:8]
        return carry

    lax.fori_loop(0, 4, attend, 0)

    greeted(friends)
    waits = []
    for d in range(1, 8):
        to = (f + d) % 8
        waits.append(links.start(st_out.at[to], st_in.at[d], me.ffn(to)))
        waits.append(links.start(o_out.at[to], o_in.at[d], me.ffn(to)))
    arrived(*waits)
    for h in range(2):
        stats = [st_out[f, h]] + [st_in[d, h] for d in range(1, 8)]
        tops = [s[0:1] for s in stats]
        top = functools.reduce(jnp.maximum, tops)
        weights = [s[1:2] * jnp.exp2((m - top) * SCALE) for s, m in zip(stats, tops)]
        total = sum(weights[1:], weights[0])
        shares = jnp.concatenate(
            [w / total for w in weights] + [jnp.zeros((120, 128), F32)], axis=0
        )
        shares = jnp.transpose(shares)[:SPAN]
        mine = o_out[f, h].astype(F32) * shares[:, 0:1]
        for d in range(1, 8):
            mine += o_in[d, h].astype(F32) * shares[:, d : d + 1]
        att[f, h] = mine.astype(BF16)
    arrived(*[links.start(att.at[f], att.at[f], me.ffn((f + d) % 8)) for d in range(1, 8)])

    load_wo.wait()
    attn = jnp.concatenate([att[q, h] for h in range(2) for q in range(8)], axis=1)
    part = jnp.dot(attn, wo[...], preferred_element_type=F32)
    for j in range(4):
        piece = part[:, j * 256 : (j + 1) * 256]
        part_f[j] = piece
        part_b[j] = piece.astype(BF16)
    waits = []
    for d in range(1, 4):
        to = (t + d) % 4
        waits.append(links.start(part_b.at[to], part_in.at[d - 1], me.tp(to)))
    arrived(*waits)
    h1 = part_f[t] + resid_ref[:, pl.ds(pl.multiple_of(t * 256, 256), 256)].astype(F32)
    for d in range(3):
        h1 += part_in[d].astype(F32)
    h1 = h1.astype(BF16)
    h_ref[0, z, y] = h1[:, :128]
    h_ref[1, z, y] = h1[:, 128:]

    def ring(part, whole, first, second):
        right = links.start(whole(part, z), whole(part, z), me.at_z(1))
        left = links.start(whole(part, z), whole(part, z), me.at_z(-1))
        yield
        for s in (1, 2):
            arrived(right)
            at = (z - s + 8) % 8
            right = links.start(whole(part, at), whole(part, at), me.at_z(1))
            arrived(left)
            at = (z + s) % 8
            left = links.start(whole(part, at), whole(part, at), me.at_z(-1))
            yield
        arrived(right)
        at = (z - 3 + 8) % 8
        right = links.start(first(part, at), first(part, at), me.at_z(1))
        arrived(left)
        at = (z + 3) % 8
        left = links.start(second(part, at), second(part, at), me.at_z(-1))
        yield
        arrived(right, left)

    pair = pl.ds(2 * (y // 2), 2)

    def y_first():
        one = links.start(h_ref.at[0, z, y], h_ref.at[0, z, y], me.at_y(me.ya))
        yield
        arrived(one)
        two = links.start(h_ref.at[0, z, pair], h_ref.at[0, z, pair], me.at_y(me.yb))
        yield
        arrived(two)
        yield from ring(
            0,
            lambda p, at: h_ref.at[p, at],
            lambda p, at: h_ref.at[p, at, pl.ds(0, 2)],
            lambda p, at: h_ref.at[p, at, pl.ds(2, 2)],
        )

    low, high = pl.ds(0, 48), pl.ds(48, 48)

    def z_first():
        yield from ring(
            1,
            lambda p, at: h_ref.at[p, at, y],
            lambda p, at: h_ref.at[p, at, y, low],
            lambda p, at: h_ref.at[p, at, y, high],
        )
        a = links.start(h_ref.at[1, :, y, low], h_ref.at[1, :, y, low], me.at_y(me.ya))
        b = links.start(h_ref.at[1, :, y, high], h_ref.at[1, :, y, high], me.at_y(me.yb))
        yield
        arrived(a)
        a = links.start(h_ref.at[1, :, pair, low], h_ref.at[1, :, pair, low], me.at_y(me.yb))
        arrived(b)
        b = links.start(h_ref.at[1, :, y, high], h_ref.at[1, :, y, high], me.at_y(me.ya))
        b2 = links.start(
            h_ref.at[1, :, me.yb, high], h_ref.at[1, :, me.yb, high], me.at_y(me.ya)
        )
        yield
        arrived(a, b, b2)

    in_turn(y_first(), z_first())
    links.finish()


def attention_call(lengths, prefixes, queries, new_kv, resid, kv_cache, out_weight):
    vmem = pl.BlockSpec(memory_space=pltpu.VMEM)
    smem = pl.BlockSpec(memory_space=pltpu.SMEM)
    hbm = pl.BlockSpec(memory_space=pl.ANY)
    copies = 7 * 3 + 3 + 2 + 8 + 8 + 5
    return pl.pallas_call(
        attention_kernel,
        out_shape=jax.ShapeDtypeStruct((2, 8, 4, SPAN, 128), BF16),
        in_specs=[smem, smem, vmem, vmem, vmem, hbm, hbm],
        out_specs=vmem,
        scratch_shapes=[
            pltpu.VMEM((2, KEYS, 256), BF16),
            pltpu.VMEM((2048, WIDTH), BF16),
            pltpu.VMEM((8, 2, SPAN, DH), BF16),
            pltpu.VMEM((8, 2, 8, 128), F32),
            pltpu.VMEM((8, 2, SPAN, DH), BF16),
            pltpu.VMEM((8, 2, 8, 128), F32),
            pltpu.VMEM((8, 2, SPAN, DH), BF16),
            pltpu.VMEM((4, SPAN, 256), F32),
            pltpu.VMEM((4, SPAN, 256), BF16),
            pltpu.VMEM((3, SPAN, 256), BF16),
            pltpu.SemaphoreType.DMA((3,)),
            pltpu.SemaphoreType.DMA((copies,)),
            pltpu.SemaphoreType.DMA((copies,)),
        ],
        compiler_params=pltpu.CompilerParams(
            collective_id=0, has_side_effects=True, vmem_limit_bytes=50 << 20
        ),
        name="attend_and_gather",
    )(lengths, prefixes, queries, new_kv, resid, kv_cache, out_weight)


def ffn_kernel(
    length_ref, gain_ref, h_ref, gate_hbm, up_hbm, down_hbm,
    out_ref,
    gw, uw, dw, xs, own_h, sq_out, sq_in,
    send_core, recv_core, keep, stage, recv_one, recv_two, hid,
    pa, ra_one, ra_two, qa, za, pb, zb, qb, rb_one, rb_two,
    local_sems, send_sems, recv_sems,
):
    me = Place()
    links = Links(send_sems, recv_sems)
    f, t, y, z, x, c = me.f, me.t, me.y, me.z, me.x, me.c
    load_g = pltpu.make_async_copy(gate_hbm, gw, local_sems.at[0])
    load_u = pltpu.make_async_copy(up_hbm, uw, local_sems.at[1])
    load_d = pltpu.make_async_copy(down_hbm, dw, local_sems.at[2])
    load_g.start()
    load_u.start()
    load_d.start()
    friends = [me.ffn((f + d) % 8) for d in range(1, 8)]
    friends += [me.at_y(me.ya), me.at_y(me.yb), me.at_z(1), me.at_z(-1)]
    greet(friends)

    gain = gain_ref[...].astype(F32)
    lane = lax.broadcasted_iota(jnp.int32, (SPAN, 128), 1)
    squares = jnp.zeros((SPAN, 128), F32)
    for g in range(8):
        row, side = g // 2, g % 2
        rows = jnp.concatenate(
            [h_ref[p, side * 4 + k, row] for k in range(4) for p in range(2)], axis=1
        ).astype(F32)
        squares = jnp.where(lane == g, jnp.sum(rows * rows, axis=1, keepdims=True), squares)
        xs[side, row] = (rows * gain).astype(BF16)
    mine = jnp.concatenate(
        [h_ref[p, me.zh * 4 + k, y] for k in range(4) for p in range(2)], axis=1
    )
    own_h[...] = mine.astype(F32)
    turned = jnp.transpose(jnp.concatenate([squares, jnp.zeros((32, 128), F32)], axis=0))
    for g in range(8):
        sq_out[g] = jnp.broadcast_to(turned[g : g + 1], (8, 128))

    greeted(friends)
    sq_waits = []
    for d in range(1, 8):
        to = (f + d) % 8
        sq_waits.append(links.start(sq_out.at[to], sq_in.at[d - 1], me.ffn(to)))

    load_g.wait()
    load_u.wait()
    tail = jnp.zeros((4, 2, 48, 128), F32)

    def project(side, dst):
        rows = xs[side].reshape(4 * SPAN, WIDTH)
        for k, w in enumerate((gw, uw)):
            base = k * WIDTH
            dst[:, :, :, base + 896 : base + 1024] = tail.astype(dst.dtype)
            out = jnp.dot(rows, w[...], preferred_element_type=F32)
            dst[:, :, :, base : base + HID] = out.astype(dst.dtype).reshape(4, 2, 48, HID)

    project(1 - c, send_core)
    core_waits = [
        links.start(send_core.at[i], recv_core.at[i], me.core()) for i in range(4)
    ]
    project(c, keep)
    arrived(*core_waits)

    def joined(i, half):
        return keep[i, half] + recv_core[i, half].astype(F32)

    def push(half, blocks, device):
        waits = []
        for slot, i in enumerate(blocks):
            stage[i, half] = joined(i, half).astype(BF16)
            waits.append(links.start(stage.at[i, half], recv_one.at[half, slot], device))
        return waits

    wait_a = push(0, (me.xa, 3 - me.xa), me.at_x(me.xa))
    wait_b = push(1, (me.xb, flip(me.xb)), me.at_x(me.xb))
    arrived(*wait_a)
    stage[me.xb, 0] = (joined(me.xb, 0) + recv_one[0, 1].astype(F32)).astype(BF16)
    two_a = links.start(stage.at[me.xb, 0], recv_two.at[0], me.at_x(me.xb))
    arrived(*wait_b)
    stage[me.xa, 1] = (joined(me.xa, 1) + recv_one[1, 1].astype(F32)).astype(BF16)
    two_b = links.start(stage.at[me.xa, 1], recv_two.at[1], me.at_x(me.xa))

    arrived(*sq_waits)
    total = sq_out[f]
    for d in range(7):
        total += sq_in[d]
    total = jnp.transpose(jnp.concatenate([total] * 16, axis=0))
    rs = lax.rsqrt(total / D + 1e-06)[:SPAN, 0:1]

    def activate(half):
        both = (
            joined(x, half) + recv_one[half, 0].astype(F32) + recv_two[half].astype(F32)
        )
        r = rs[half * 48 : (half + 1) * 48]
        gate, up = both[:, :WIDTH] * r, both[:, WIDTH:] * r
        hid[c, x, half] = (gate / (1.0 + jnp.exp(-gate)) * up).astype(BF16)

    def share(where, device):
        return links.start(hid.at[where], hid.at[where], device)

    arrived(two_a)
    activate(0)
    one_a = share((c, x, 0), me.at_x(me.xa))
    core_waits = [share((c, x, 0), me.core())]
    arrived(two_b)
    activate(1)
    one_b = share((c, x, 1), me.at_x(me.xb))
    core_waits.append(share((c, x, 1), me.core()))
    arrived(one_a)
    x_pair = pl.ds(2 * (x // 2), 2)
    two_a = share((c, x_pair, 0), me.at_x(me.xb))
    core_waits.append(share((c, me.xa, 0), me.core()))
    arrived(one_b)
    two_b = share((c, x, 1), me.at_x(me.xa))
    two_c = share((c, me.xb, 1), me.at_x(me.xa))
    core_waits.append(share((c, me.xb, 1), me.core()))
    arrived(two_a)
    far_pair = pl.ds(2 - 2 * (x // 2), 2)
    core_waits.append(share((c, far_pair, 0), me.core()))
    arrived(two_b, two_c)
    core_waits.append(share((c, me.xa, 1), me.core()))
    core_waits.append(share((c, flip(me.xb), 1), me.core()))

    load_d.wait()

    def lower(side):
        rows = hid[side].reshape(4 * SPAN, WIDTH)[:, :HID]
        out = jnp.dot(rows, dw[...], preferred_element_type=F32)
        for i in range(4):
            for k in range(4):
                base = i * SPAN + k * ROWS_OUT
                piece = out[base : base + ROWS_OUT].astype(BF16)
                for j in range(2):
                    pa[j, i, side * 4 + k] = piece[:, j * 256 : (j + 1) * 256]
                    pb[side * 4 + k, j, i] = piece[:, 512 + j * 256 : 768 + j * 256]

    lower(c)
    arrived(*core_waits)
    lower(1 - c)

    def plus(*parts):
        out = parts[0].astype(F32)
        for part in parts[1:]:
            out += part.astype(F32)
        return out

    def y_stage(src, one, two):
        wait = [[], []]
        for slot, i in enumerate((me.ya, 3 - me.ya)):
            wait[0].append(links.start(src.at[0, i], one.at[0, slot], me.at_y(me.ya)))
        for slot, i in enumerate((me.yb, flip(me.yb))):
            wait[1].append(links.start(src.at[1, i], one.at[1, slot], me.at_y(me.yb)))
        yield
        yield
        arrived(*wait[0])
        src[0, me.yb] = plus(src[0, me.yb], one[0, 1]).astype(BF16)
        a = links.start(src.at[0, me.yb], two.at[0], me.at_y(me.yb))
        arrived(*wait[1])
        src[1, me.ya] = plus(src[1, me.ya], one[1, 1]).astype(BF16)
        b = links.start(src.at[1, me.ya], two.at[1], me.at_y(me.ya))
        yield
        arrived(a, b)

    def z_stage(src, got):
        far = (z + 4) % 8
        right = links.start(src.at[far, 0], got.at[0, 0, 0], me.at_z(1))
        left = links.start(src.at[far, 1], got.at[1, 0, 1], me.at_z(-1))
        yield
        for s in (1, 2, 3):
            at = (z + 4 - s) % 8
            arrived(right)
            if s == 1:
                src[at, 0] = plus(src[at, 0], got[0, 0, 0]).astype(BF16)
            else:
                src[at] = plus(src[at], got[0, s - 1]).astype(BF16)
            right = links.start(src.at[at], got.at[0, s], me.at_z(1))
            at = (z + 4 + s) % 8
            arrived(left)
            if s == 1:
                src[at, 1] = plus(src[at, 1], got[1, 0, 1]).astype(BF16)
            else:
                src[at] = plus(src[at], got[1, s - 1]).astype(BF16)
            left = links.start(src.at[at], got.at[1, s], me.at_z(-1))
            yield
        arrived(right, left)

    def y_first():
        yield from y_stage(pa, ra_one, ra_two)
        for j in range(2):
            qa[:, j] = plus(pa[j, y], ra_one[j, 0], ra_two[j]).astype(BF16)
        yield from z_stage(qa, za)

    def z_first():
        yield from z_stage(pb, zb)
        qb[...] = plus(pb[z], zb[0, 3], zb[1, 3]).astype(BF16)
        yield from y_stage(qb, rb_one, rb_two)

    in_turn(y_first(), z_first())
    left = plus(qa[z], za[0, 3], za[1, 3])
    right = [plus(qb[j, y], rb_one[j, 0], rb_two[j]) for j in range(2)]
    down = jnp.concatenate([left[0], left[1], right[0], right[1]], axis=1)
    start = pl.multiple_of(t * ROWS_OUT, 8)
    out = own_h[pl.ds(start, ROWS_OUT), :] + down
    live = start + lax.broadcasted_iota(jnp.int32, (ROWS_OUT, WIDTH), 0) < length_ref[0]
    out_ref[...] = jnp.where(live, out, 0.0).astype(BF16)
    links.finish()


def ffn_call(lengths, gain, h, gate_weight, up_weight, down_weight):
    vmem = pl.BlockSpec(memory_space=pltpu.VMEM)
    smem = pl.BlockSpec(memory_space=pltpu.SMEM)
    hbm = pl.BlockSpec(memory_space=pl.ANY)
    copies = 7 + 4 + 4 + 2 + 2 + 3 + 7 + 2 * 6 + 2 * 8
    piece = (ROWS_OUT, 256)
    return pl.pallas_call(
        ffn_kernel,
        out_shape=jax.ShapeDtypeStruct((ROWS_OUT, WIDTH), BF16),
        in_specs=[smem, vmem, vmem, hbm, hbm, hbm],
        out_specs=vmem,
        scratch_shapes=[
            pltpu.VMEM((WIDTH, HID), BF16),
            pltpu.VMEM((WIDTH, HID), BF16),
            pltpu.VMEM((HID, WIDTH), BF16),
            pltpu.VMEM((2, 4, SPAN, WIDTH), BF16),
            pltpu.VMEM((SPAN, WIDTH), F32),
            pltpu.VMEM((8, 8, 128), F32),
            pltpu.VMEM((7, 8, 128), F32),
            pltpu.VMEM((4, 2, 48, 2 * WIDTH), BF16),
            pltpu.VMEM((4, 2, 48, 2 * WIDTH), BF16),
            pltpu.VMEM((4, 2, 48, 2 * WIDTH), F32),
            pltpu.VMEM((4, 2, 48, 2 * WIDTH), BF16),
            pltpu.VMEM((2, 2, 48, 2 * WIDTH), BF16),
            pltpu.VMEM((2, 48, 2 * WIDTH), BF16),
            pltpu.VMEM((2, 4, 2, 48, WIDTH), BF16),
            pltpu.VMEM((2, 4, 8) + piece, BF16),
            pltpu.VMEM((2, 2, 8) + piece, BF16),
            pltpu.VMEM((2, 8) + piece, BF16),
            pltpu.VMEM((8, 2) + piece, BF16),
            pltpu.VMEM((2, 4, 2) + piece, BF16),
            pltpu.VMEM((8, 2, 4) + piece, BF16),
            pltpu.VMEM((2, 4, 2, 4) + piece, BF16),
            pltpu.VMEM((2, 4) + piece, BF16),
            pltpu.VMEM((2, 2) + piece, BF16),
            pltpu.VMEM((2,) + piece, BF16),
            pltpu.SemaphoreType.DMA((3,)),
            pltpu.SemaphoreType.DMA((copies,)),
            pltpu.SemaphoreType.DMA((copies,)),
        ],
        compiler_params=pltpu.CompilerParams(
            collective_id=1, has_side_effects=True, vmem_limit_bytes=56 << 20
        ),
        name="feed_forward",
    )(lengths, gain, h, gate_weight, up_weight, down_weight)


def body(
    queries,
    new_kv,
    kv_cache,
    lengths,
    prefixes,
    resid,
    out_weight,
    gain,
    gate_weight,
    up_weight,
    down_weight,
):
    h = attention_call(lengths, prefixes, queries, new_kv, resid, kv_cache, out_weight)
    return ffn_call(lengths, gain.reshape(1, -1), h, gate_weight, up_weight, down_weight)


def solution(mesh):
    return jax.shard_map(
        body,
        mesh=mesh,
        in_specs=(
            P("grp", "tp"),
            P(None, "grp", "tp"),
            P(None, "grp", "ffn", "tp"),
            P("grp"),
            P("grp"),
            P("grp", "ffn"),
            P("tp", "ffn"),
            P("ffn"),
            P("ffn", ("grp", "tp")),
            P("ffn", ("grp", "tp")),
            P(("grp", "tp"), "ffn"),
        ),
        out_specs=P(("grp", "tp"), "ffn"),
        check_vma=False,
    )
```

time: 560 us -> 141 us (0.25)
  waiting for transfers between devices: 432 us -> 0 us
  Pallas kernels: 0 us -> 125 us
  blocking collectives: 35.7 us -> 0 us
  matrix products: 30 us -> 0 us
  other arithmetic: 23.3 us -> 0 us
  between operations: 14.1 us -> 1.33 us
  local copies, waits for them, and re-layouts: 21.3 us -> 13.1 us
    reduce_scatter x1 -> x0, waiting for transfers between devices: 222 us -> none  [body(): lax.psum_scatter(jnp.dot(hidden, down_weight, preferred_element_type=jnp....]
    pallas_call x0 -> x2, Pallas kernels: none -> 125 us  [the longest x1 63.5 us: ffn_call(): pl.pallas_call(ffn_kernel, out_shape=jax.ShapeDtypeStruct((ROWS_OUT, WIDT...]
    psum x2 -> x0, waiting for transfers between devices: 120 us -> none  [the longest x1 68.5 us: body(): gate, upper, squares = lax.psum((gate, upper, squares), 'ffn')]
    all_gather x2 -> x0, waiting for transfers between devices: 89.1 us -> none  [the longest x1 69 us: body(): all_rows = lax.all_gather(h1, 'grp', axis=0, tiled=True)]
    dot_general x14 -> x0, matrix products: 30 us -> none  [the longest x5 8.54 us: update(): jnp.einsum('hrk,hkd->hrd', probs, values.astype(jnp.float32))]
    all_gather x2 -> x0, blocking collectives: 25.6 us -> none  [merged(): everything = jax.tree.map(lambda part: lax.all_gather(part, axis), x)]
    add x18 -> x0, other arithmetic: 12.9 us -> none  [the longest x7 12.6 us: combine_parts(): values = first[2] * left[..., None] + second[2] * right[..., None]]
    unnamed x11 -> x13, local copies, waits for them, and re-layouts: 1.09 us -> 11.8 us
  transfers between devices with their start and end apart: 5 -> 0, of which waited for: 5 -> 0; matrix products, arithmetic and copies ran while one was open for 0% -> 0% of each run, Pallas kernels for 0% -> 0%
where the time goes in v1:
time: 141 us; the launch traced here: 139 us
  Pallas kernels  125 us (89%)
  local copies, waits for them, and re-layouts  13.1 us (9%)
    pallas_call x1, Pallas kernels, ffn_call(): pl.pallas_call(ffn_kernel, out_shape=jax.ShapeDtypeStruct((ROWS_OUT, WIDT...  63.5 us
    pallas_call x1, Pallas kernels, attention_call(): pl.pallas_call(attention_kernel, out_shape=jax.ShapeDtypeStruct((2, 8, 4,...  61.1 us
    unnamed x13, local copies, waits for them, and re-layouts  11.8 us

profile of v1, /device:TPU:2, one launch (start us, length us, event | category | flops | bytes accessed | tf_op | source)
XLA Modules:
  0.0 139.0 jit_solution(8608589942631431845)
XLA Ops:
  1.3 1.3 reshape.3.gain_ref
  2.6 0.0 copy-start.1
  2.6 1.0 copy-done.1
  3.6 0.0 copy-start.2
  3.6 0.9 copy-done.2
  4.5 0.0 copy-start.3
  4.5 0.9 copy-done.3
  5.4 0.0 copy-start.4
  5.4 61.1 %attend_and_gather.1.h_ref = bf16[2,8,4,96,128]{4,3,2,1,0:T(8,128)(2,1)S(1)} custom-call(s32[1]{0:T(128)S(6)} %copy.15.length_ref, s32[1]{0:T(128)S(6)} %copy.16.prefix_ref, bf16[96,2048]{1,0:T(8,128)(2,1)S(1)} %copy-done.1, bf16[2,96,256]{2,1,0:T(8,128)(2,1)S(1)} %copy-done.3, bf16[96,1024]{1,0:T(8,128)(2,1)S(1)} %copy-done.2, ...), custom_call_target="tpu_custom_call" | custom-call | tf_op jit(solution)/shard_map/attend_and_gather/pallas_call | solution.py:289
  66.5 0.0 copy-start
  66.6 1.2 copy-done
  67.7 0.0 copy-done.4
  67.7 2.5 %copy.12.gate_hbm = bf16[1024,924]{1,0:T(8,128)(2,1)} copy(bf16[1024,924]{0,1:T(8,128)(2,1)S(1)} %copy-done.4) | data formatting | bytes 3784704 | tf_op args[8]
  70.2 3.8 %copy.13.up_hbm = bf16[1024,924]{1,0:T(8,128)(2,1)} copy(bf16[1024,924]{0,1:T(8,128)(2,1)} %param.20) | data formatting | bytes 3784704 | tf_op args[9]
  74.1 63.5 %feed_forward.1 = bf16[24,1024]{1,0:T(8,128)(2,1)} custom-call(s32[1]{0:T(128)S(6)} %copy.15.length_ref, bf16[1,1024]{1,0:T(2,128)(2,1)} %reshape.3.gain_ref, bf16[2,8,4,96,128]{4,3,2,1,0:T(8,128)(2,1)} %copy-done, bf16[1024,924]{1,0:T(8,128)(2,1)} %copy.12.gate_hbm, bf16[1024,924]{1,0:T(8,128)(2,1)} %copy.13.up_hbm, bf16[924,1024]{1,0:T(8,128)(2,1)} %down_hbm.1), custom_call_target="tpu_custom_call" | custom-call | tf_op jit(solution)/shard_map/feed_forward/pallas_call | solution.py:531
  137.6 1.4 %copy.17 = bf16[24,1024]{1,0:T(8,128)(2,1)} copy(bf16[24,1024]{1,0:T(8,128)(2,1)} %feed_forward.1) | data formatting | bytes 98304
Async XLA Ops:
  2.6 1.0 copy-start.1
  3.6 0.9 copy-start.2
  4.5 0.9 copy-start.3
  5.4 62.3 %copy-start.4 = (bf16[1024,924]{0,1:T(8,128)(2,1)S(1)}, bf16[1024,924]{0,1:T(8,128)(2,1)}, u32[]{:S(2)}) copy-start(bf16[1024,924]{0,1:T(8,128)(2,1)} %param.19) | copy-start | bytes 5677060
  66.5 1.2 copy-start

commit v2 on v1

v2 whole, which is shorter than its diff:
```python
import functools
import math

import jax
import jax.numpy as jnp
from jax import lax
from jax.experimental import pallas as pl
from jax.experimental.pallas import tpu as pltpu
from jax.sharding import PartitionSpec as P

MESH = pl.DeviceIdType.MESH
F32 = jnp.float32
BF16 = jnp.bfloat16

D = 8192
DH = 128
SPAN = 96
ROWS_OUT = 24
MAIN = 896
REST = 28
BOTH = 1920
KEYS = 2048
WIDTH = 1024
HID = 924
NEG = -1e30
SCALE = math.log2(math.e) / math.sqrt(DH)


class Place:
    def __init__(self):
        g = lax.axis_index("grp")
        self.t = lax.axis_index("tp")
        self.f = lax.axis_index("ffn")
        self.y, self.zh = g // 2, g % 2
        self.x, self.c = self.f // 2, self.f % 2
        self.z = self.zh * 4 + self.t
        self.xa, self.xb = flip(self.x), 3 - self.x
        self.ya, self.yb = flip(self.y), 3 - self.y

    def ffn(self, f):
        return {"ffn": f}

    def tp(self, t):
        return {"tp": t}

    def core(self):
        return {"ffn": self.x * 2 + 1 - self.c}

    def at_x(self, x):
        return {"ffn": x * 2 + self.c}

    def at_y(self, y):
        return {"grp": y * 2 + self.zh}

    def at_y_step(self, step):
        return self.at_y((self.y + step) % 4)

    def at_z(self, step):
        z = (self.z + step + 8) % 8
        return {"grp": self.y * 2 + z // 4, "tp": z % 4}


def flip(v):
    return v + 1 - 2 * (v % 2)


class Links:
    def __init__(self, send_sems, recv_sems):
        self.send_sems, self.recv_sems = send_sems, recv_sems
        self.started = []

    def start(self, src, dst, device):
        k = len(self.started)
        copy = pltpu.make_async_remote_copy(
            src_ref=src,
            dst_ref=dst,
            send_sem=self.send_sems.at[k],
            recv_sem=self.recv_sems.at[k],
            device_id=device,
            device_id_type=MESH,
        )
        copy.start()
        self.started.append(copy)
        return copy

    def finish(self):
        for copy in self.started:
            copy.wait_send()


def greet(devices):
    barrier = pltpu.get_barrier_semaphore()
    for device in devices:
        pl.semaphore_signal(barrier, inc=1, device_id=device, device_id_type=MESH)


def greeted(devices):
    pl.semaphore_wait(pltpu.get_barrier_semaphore(), len(devices))


def in_turn(*flows):
    alive = list(flows)
    while alive:
        for flow in list(alive):
            try:
                next(flow)
            except StopIteration:
                alive.remove(flow)


def arrived(*copies):
    for copy in copies:
        copy.wait_recv()


NT = (((1,), (1,)), ((), ()))


def plus(*parts):
    out = parts[0].astype(F32)
    for part in parts[1:]:
        out += part.astype(F32)
    return out


def layer_kernel(
    length_ref, prefix_ref, gain_ref,
    q_hbm, new_hbm, resid_hbm, cache_hbm, wo_hbm, gate_hbm, up_hbm, down_hbm,
    out_ref,
    q_ref, new_ref, resid_ref, kv, wo, gw, uw, rw, dw,
    o_out, st_out, o_in, st_in, att, part_f, part_b, part_in, h_ref,
    xs, own_h, sq_out, sq_in,
    send_core, recv_core, keep, stage, recv_one, recv_two, hid,
    pieces, from_y, summed, za, zb, done, last,
    local_sems, send_sems, recv_sems,
):
    me = Place()
    links = Links(send_sems, recv_sems)
    f, t, y, z, x, c = me.f, me.t, me.y, me.z, me.x, me.c

    def load(k, src, dst):
        copy = pltpu.make_async_copy(src, dst, local_sems.at[k])
        copy.start()
        return copy

    first = [
        load(0, q_hbm, q_ref),
        load(1, cache_hbm.at[0, 0], kv.at[0]),
        load(2, new_hbm, new_ref),
        load(3, cache_hbm.at[1, 0], kv.at[1]),
    ]
    friends = [me.ffn((f + d) % 8) for d in range(1, 8)]
    friends += [me.tp((t + d) % 4) for d in range(1, 4)]
    friends += [me.at_y_step(d) for d in range(1, 4)]
    friends += [me.at_z(1), me.at_z(-1)]
    greet(friends)

    length, prefix = length_ref[0], prefix_ref[0]
    lanes = lax.broadcasted_iota(jnp.int32, (1, KEYS), 1)
    bias = jnp.where(f * KEYS + lanes < prefix, 0.0, NEG).astype(F32)
    slot = lax.broadcasted_iota(jnp.int32, (SPAN, SPAN), 0)
    key = lax.broadcasted_iota(jnp.int32, (SPAN, SPAN), 1)
    limit = jnp.where(f == 0, length, 0)
    new_bias = jnp.where((key <= slot) & (key < limit), 0.0, NEG).astype(F32)
    new_bias = jnp.concatenate([new_bias] * 4, axis=0)
    lane = lax.broadcasted_iota(jnp.int32, (4 * SPAN, 128), 1)
    for copy in first:
        copy.wait()
    load_wo = load(4, wo_hbm, wo)
    load_r = load(5, resid_hbm, resid_ref)
    load_g = load(6, gate_hbm, gw)
    load_u = load(7, up_hbm, uw)
    load_d = load(8, down_hbm, dw)

    def attend(step, carry):
        half, h = step // 2, step % 2
        cols = pl.ds(pl.multiple_of(h * DH, DH), DH)
        keys, values = kv[0, :, cols], kv[1, :, cols]
        new_keys, new_values = new_ref[0, :, cols], new_ref[1, :, cols]
        q = jnp.concatenate(
            [
                q_ref[:, pl.ds(pl.multiple_of((h * 8 + half * 4 + i) * DH, DH), DH)]
                for i in range(4)
            ],
            axis=0,
        )
        s = lax.dot_general(q, keys, NT, preferred_element_type=F32) + bias
        s_new = lax.dot_general(q, new_keys, NT, preferred_element_type=F32) + new_bias
        top = jnp.maximum(
            jnp.max(s, axis=1, keepdims=True), jnp.max(s_new, axis=1, keepdims=True)
        )
        p = jnp.exp2((s - top) * SCALE).astype(BF16)
        p_new = jnp.exp2((s_new - top) * SCALE).astype(BF16)
        wide = jnp.concatenate([values, jnp.ones((KEYS, DH), BF16)], axis=1)
        wide_new = jnp.concatenate([new_values, jnp.ones((SPAN, DH), BF16)], axis=1)
        acc = jnp.dot(p, wide, preferred_element_type=F32) + jnp.dot(
            p_new, wide_new, preferred_element_type=F32
        )
        total = acc[:, DH:]
        out = (acc[:, :DH] / total).astype(BF16)
        stats = jnp.where(lane == 0, top, jnp.where(lane == 1, total, 0.0))
        for i in range(4):
            rows = slice(i * SPAN, (i + 1) * SPAN)
            o_out[half * 4 + i, h] = out[rows]
            square = jnp.concatenate([stats[rows], jnp.zeros((32, 128), F32)], axis=0)
            st_out[half * 4 + i, h] = jnp.transpose(square)[:8]
        return carry

    lax.fori_loop(0, 4, attend, 0)

    greeted(friends)
    waits = []
    for d in range(1, 8):
        to = (f + d) % 8
        waits.append(links.start(st_out.at[to], st_in.at[d], me.ffn(to)))
        waits.append(links.start(o_out.at[to], o_in.at[d], me.ffn(to)))
    arrived(*waits)
    for h in range(2):
        stats = [st_out[f, h]] + [st_in[d, h] for d in range(1, 8)]
        tops = [s[0:1] for s in stats]
        top = functools.reduce(jnp.maximum, tops)
        weights = [s[1:2] * jnp.exp2((m - top) * SCALE) for s, m in zip(stats, tops)]
        total = sum(weights[1:], weights[0])
        shares = jnp.concatenate(
            [w / total for w in weights] + [jnp.zeros((120, 128), F32)], axis=0
        )
        shares = jnp.transpose(shares)[:SPAN]
        mine = o_out[f, h].astype(F32) * shares[:, 0:1]
        for d in range(1, 8):
            mine += o_in[d, h].astype(F32) * shares[:, d : d + 1]
        att[f, h] = mine.astype(BF16)
    waits = [links.start(att.at[f], att.at[f], me.ffn((f + d) % 8)) for d in range(1, 8)]

    load_wo.wait()
    load_r.wait()
    load_g.wait()
    load_u.wait()
    rw[...] = jnp.zeros((128, WIDTH), BF16)
    rw[0:REST] = gw[MAIN:HID]
    rw[64 : 64 + REST] = uw[MAIN:HID]
    arrived(*waits)
    attn = jnp.concatenate([att[q, h] for h in range(2) for q in range(8)], axis=1)
    part = jnp.dot(attn, wo[...], preferred_element_type=F32)
    for j in range(4):
        piece = part[:, j * 256 : (j + 1) * 256]
        part_f[j] = piece
        part_b[j] = piece.astype(BF16)
    waits = []
    for d in range(1, 4):
        to = (t + d) % 4
        waits.append(links.start(part_b.at[to], part_in.at[d - 1], me.tp(to)))
    arrived(*waits)
    h1 = part_f[t] + resid_ref[:, pl.ds(pl.multiple_of(t * 256, 256), 256)].astype(F32)
    for d in range(3):
        h1 += part_in[d].astype(F32)
    h1 = h1.astype(BF16)
    h_ref[0, z, y] = h1[:, :128]
    h_ref[1, z, y] = h1[:, 128:]

    def pass_on(ref, device):
        return links.start(ref, ref, device)

    def ring(p, row, seen):
        right = pass_on(h_ref.at[p, z, row], me.at_z(1))
        left = pass_on(h_ref.at[p, z, row], me.at_z(-1))
        yield
        for s in (1, 2, 3):
            rows = (pl.ds(0, SPAN), pl.ds(0, SPAN)) if s < 3 else (pl.ds(0, 48), pl.ds(48, 48))
            at = (z - s + 8) % 8
            arrived(right)
            right = pass_on(h_ref.at[p, at, row, rows[0]], me.at_z(1))
            seen(at)
            at = (z + s) % 8
            arrived(left)
            left = pass_on(h_ref.at[p, at, row, rows[1]], me.at_z(-1))
            seen(at)
            yield
        arrived(right, left)
        seen((z + 4) % 8)

    def from_peer(d):
        copy = pass_on(h_ref.at[0, z, y], me.at_y_step(d))
        yield
        arrived(copy)
        yield from ring(0, (y + 4 - d) % 4, lambda at: None)

    def own_then_peers():
        waits = []

        def seen(at):
            for d in (1, 2, 3):
                waits.append(pass_on(h_ref.at[1, at, y], me.at_y_step(d)))

        seen(z)
        yield from ring(1, y, seen)
        yield
        arrived(*waits)

    in_turn(
        ring(0, y, lambda at: None),
        from_peer(1),
        from_peer(3),
        from_peer(2),
        own_then_peers(),
    )

    gain = gain_ref[...].astype(F32).reshape(1, WIDTH)
    lane = lax.broadcasted_iota(jnp.int32, (SPAN, 128), 1)
    squares = jnp.zeros((SPAN, 128), F32)

    def rows_of(side, row):
        return jnp.concatenate(
            [h_ref[p, side * 4 + k, row] for k in range(4) for p in range(2)], axis=1
        ).astype(F32)

    for g in range(8):
        rows = rows_of(g % 2, g // 2)
        squares = jnp.where(lane == g, jnp.sum(rows * rows, axis=1, keepdims=True), squares)
        xs[g % 2, g // 2] = (rows * gain).astype(BF16)

    def project(side, dst):
        rows = xs[side].reshape(4 * SPAN, WIDTH)
        for w, base, size in ((gw, 0, MAIN), (uw, MAIN, MAIN), (rw, 2 * MAIN, 128)):
            out = lax.dot_general(rows, w[0:size], NT, preferred_element_type=F32)
            dst[:, :, :, base : base + size] = out.astype(dst.dtype).reshape(4, 2, 48, size)

    project(1 - c, send_core)
    core_waits = [
        links.start(send_core.at[i], recv_core.at[i], me.core()) for i in range(4)
    ]
    turned = jnp.transpose(jnp.concatenate([squares, jnp.zeros((32, 128), F32)], axis=0))
    for g in range(8):
        sq_out[g] = jnp.broadcast_to(turned[g : g + 1], (8, 128))
    sq_waits = []
    for d in range(1, 8):
        to = (f + d) % 8
        sq_waits.append(links.start(sq_out.at[to], sq_in.at[d - 1], me.ffn(to)))
    project(c, keep)
    arrived(*core_waits)

    def joined(i, half):
        return keep[i, half] + recv_core[i, half].astype(F32)

    def push(half, slot, i, device):
        stage[i, half] = joined(i, half).astype(BF16)
        return links.start(stage.at[i, half], recv_one.at[half, slot], device)

    far_a = push(0, 1, 3 - me.xa, me.at_x(me.xa))
    far_b = push(1, 1, flip(me.xb), me.at_x(me.xb))
    near_a = push(0, 0, me.xa, me.at_x(me.xa))
    near_b = push(1, 0, me.xb, me.at_x(me.xb))
    own_h[...] = rows_of(me.zh, y)
    arrived(far_a)
    stage[me.xb, 0] = (joined(me.xb, 0) + recv_one[0, 1].astype(F32)).astype(BF16)
    two_a = links.start(stage.at[me.xb, 0], recv_two.at[0], me.at_x(me.xb))
    arrived(far_b)
    stage[me.xa, 1] = (joined(me.xa, 1) + recv_one[1, 1].astype(F32)).astype(BF16)
    two_b = links.start(stage.at[me.xa, 1], recv_two.at[1], me.at_x(me.xa))

    arrived(*sq_waits)
    total = sq_out[f]
    for d in range(7):
        total += sq_in[d]
    total = jnp.transpose(jnp.concatenate([total] * 16, axis=0))
    rs = lax.rsqrt(total / D + 1e-06)[:SPAN, 0:1]

    def silu(v):
        return v / (1.0 + jnp.exp(-v))

    def activate(half):
        both = plus(joined(x, half), recv_one[half, 0], recv_two[half])
        both = both * rs[half * 48 : (half + 1) * 48]
        rest = both[:, 2 * MAIN :]
        hid[c, x, half, :, 0:MAIN] = (silu(both[:, :MAIN]) * both[:, MAIN : 2 * MAIN]).astype(BF16)
        hid[c, x, half, :, MAIN:] = (silu(rest) * pltpu.roll(rest, 64, 1)).astype(BF16)

    def share(half, i, device):
        return pass_on(hid.at[c, i, half], device)

    arrived(near_a, two_a)
    activate(0)
    a0 = share(0, x, me.at_x(me.xa))
    b0 = share(0, x, me.at_x(me.xb))
    core_waits = [share(0, x, me.core())]
    arrived(near_b, two_b)
    activate(1)
    b1 = share(1, x, me.at_x(me.xb))
    a1 = share(1, x, me.at_x(me.xa))
    core_waits.append(share(1, x, me.core()))
    arrived(a0)
    far_0 = share(0, me.xa, me.at_x(me.xb))
    core_waits.append(share(0, me.xa, me.core()))
    arrived(b1)
    far_1 = share(1, me.xb, me.at_x(me.xa))
    core_waits.append(share(1, me.xb, me.core()))
    arrived(b0)
    core_waits.append(share(0, me.xb, me.core()))
    arrived(a1)
    core_waits.append(share(1, me.xa, me.core()))
    load_d.wait()
    arrived(far_0)
    core_waits.append(share(0, flip(me.xb), me.core()))
    arrived(far_1)
    core_waits.append(share(1, flip(me.xb), me.core()))

    def lower(side):
        rows = hid[side].reshape(4 * SPAN, WIDTH)[:, :HID]
        out = jnp.dot(rows, dw[...], preferred_element_type=F32)
        for i in range(4):
            for k in range(4):
                base = i * SPAN + k * ROWS_OUT
                piece = out[base : base + ROWS_OUT].astype(BF16)
                for j in range(4):
                    pieces[j // 2, side * 4 + k, i, j % 2] = piece[:, j * 256 : (j + 1) * 256]

    lower(c)
    arrived(*core_waits)
    lower(1 - c)

    def z_stage(src, got):
        far = (z + 4) % 8
        right = links.start(src(far).at[0], got.at[0, 0, 0], me.at_z(1))
        left = links.start(src(far).at[1], got.at[1, 0, 1], me.at_z(-1))
        yield
        for s in (1, 2, 3):
            for way, at in ((0, (z + 4 - s) % 8), (1, (z + 4 + s) % 8)):
                ref = src(at)
                arrived(left if way else right)
                if s == 1:
                    ref[way] = plus(ref[way], got[way, 0, way]).astype(BF16)
                else:
                    ref[...] = plus(ref[...], got[way, s - 1]).astype(BF16)
                if way:
                    left = links.start(ref, got.at[1, s], me.at_z(-1))
                else:
                    right = links.start(ref, got.at[0, s], me.at_z(1))
            yield
        arrived(right, left)

    def y_first():
        waits = {}
        for s in (4, 3, 5, 2, 6, 1, 7, 0):
            at = (z + s) % 8
            waits[s] = [
                links.start(
                    pieces.at[0, at, (y + d) % 4], from_y.at[d - 1, at], me.at_y_step(d)
                )
                for d in (1, 3, 2)
            ]
        yield
        ready = set()

        def src(at_step):
            at = (z + at_step) % 8
            if at_step not in ready:
                arrived(*waits[at_step])
                summed[at] = plus(
                    pieces[0, at, y], from_y[0, at], from_y[1, at], from_y[2, at]
                ).astype(BF16)
                ready.add(at_step)
            return summed.at[at]

        far = src(4)
        right = links.start(far.at[0], za.at[0, 0, 0], me.at_z(1))
        left = links.start(far.at[1], za.at[1, 0, 1], me.at_z(-1))
        src(3)
        src(5)
        yield
        for s in (1, 2, 3):
            for way, step in ((0, 4 - s), (1, 4 + s)):
                ref = src(step)
                arrived(left if way else right)
                if s == 1:
                    ref[way] = plus(ref[way], za[way, 0, way]).astype(BF16)
                else:
                    ref[...] = plus(ref[...], za[way, s - 1]).astype(BF16)
                if way:
                    left = links.start(ref, za.at[1, s], me.at_z(-1))
                else:
                    right = links.start(ref, za.at[0, s], me.at_z(1))
            yield
        src(0)
        arrived(right, left)

    def z_first(d):
        row = (y + d) % 4
        got = zb.at[d]
        yield from z_stage(lambda at: pieces.at[1, at, row], got)
        if d:
            done[d - 1] = plus(pieces[1, z, row], got[0, 3], got[1, 3]).astype(BF16)
            copy = links.start(done.at[d - 1], last.at[d - 1], me.at_y_step(d))
            yield
            arrived(copy)

    in_turn(y_first(), z_first(2), z_first(1), z_first(3), z_first(0))
    left = plus(summed[z], za[0, 3], za[1, 3])
    right = plus(pieces[1, z, y], zb[0, 0, 3], zb[0, 1, 3], last[0], last[1], last[2])
    down = jnp.concatenate([left[0], left[1], right[0], right[1]], axis=1)
    start = pl.multiple_of(t * ROWS_OUT, 8)
    out = own_h[pl.ds(start, ROWS_OUT), :] + down
    live = start + lax.broadcasted_iota(jnp.int32, (ROWS_OUT, WIDTH), 0) < length
    out_ref[...] = jnp.where(live, out, 0.0).astype(BF16)
    links.finish()


def layer_call(*args):
    vmem = pl.BlockSpec(memory_space=pltpu.VMEM)
    smem = pl.BlockSpec(memory_space=pltpu.SMEM)
    hbm = pl.BlockSpec(memory_space=pl.ANY)
    copies = 14 + 7 + 3 + 40 + 3 + 24 + 4 + 7 + 6 + 14 + 24 + 8 + 32 + 3
    piece = (2, ROWS_OUT, 256)
    block = (4, 2, 48, BOTH)
    return pl.pallas_call(
        layer_kernel,
        out_shape=jax.ShapeDtypeStruct((ROWS_OUT, WIDTH), BF16),
        in_specs=[smem, smem, vmem] + [hbm] * 8,
        out_specs=vmem,
        scratch_shapes=[
            pltpu.VMEM((SPAN, 2048), BF16),
            pltpu.VMEM((2, SPAN, 256), BF16),
            pltpu.VMEM((SPAN, WIDTH), BF16),
            pltpu.VMEM((2, KEYS, 256), BF16),
            pltpu.VMEM((2048, WIDTH), BF16),
            pltpu.VMEM((HID, WIDTH), BF16),
            pltpu.VMEM((HID, WIDTH), BF16),
            pltpu.VMEM((128, WIDTH), BF16),
            pltpu.VMEM((HID, WIDTH), BF16),
            pltpu.VMEM((8, 2, SPAN, DH), BF16),
            pltpu.VMEM((8, 2, 8, 128), F32),
            pltpu.VMEM((8, 2, SPAN, DH), BF16),
            pltpu.VMEM((8, 2, 8, 128), F32),
            pltpu.VMEM((8, 2, SPAN, DH), BF16),
            pltpu.VMEM((4, SPAN, 256), F32),
            pltpu.VMEM((4, SPAN, 256), BF16),
            pltpu.VMEM((3, SPAN, 256), BF16),
            pltpu.VMEM((2, 8, 4, SPAN, 128), BF16),
            pltpu.VMEM((2, 4, SPAN, WIDTH), BF16),
            pltpu.VMEM((SPAN, WIDTH), F32),
            pltpu.VMEM((8, 8, 128), F32),
            pltpu.VMEM((7, 8, 128), F32),
            pltpu.VMEM(block, BF16),
            pltpu.VMEM(block, BF16),
            pltpu.VMEM(block, F32),
            pltpu.VMEM(block, BF16),
            pltpu.VMEM((2, 2, 48, BOTH), BF16),
            pltpu.VMEM((2, 48, BOTH), BF16),
            pltpu.VMEM((2, 4, 2, 48, WIDTH), BF16),
            pltpu.VMEM((2, 8, 4) + piece, BF16),
            pltpu.VMEM((3, 8) + piece, BF16),
            pltpu.VMEM((8,) + piece, BF16),
            pltpu.VMEM((2, 4) + piece, BF16),
            pltpu.VMEM((4, 2, 4) + piece, BF16),
            pltpu.VMEM((3,) + piece, BF16),
            pltpu.VMEM((3,) + piece, BF16),
            pltpu.SemaphoreType.DMA((9,)),
            pltpu.SemaphoreType.DMA((copies,)),
            pltpu.SemaphoreType.DMA((copies,)),
        ],
        compiler_params=pltpu.CompilerParams(
            collective_id=0, has_side_effects=True, vmem_limit_bytes=60 << 20
        ),
        name="layer",
    )(*args)


def body(
    queries,
    new_kv,
    kv_cache,
    lengths,
    prefixes,
    resid,
    out_weight,
    gain,
    gate_weight,
    up_weight,
    down_weight,
):
    return layer_call(
        lengths,
        prefixes,
        gain,
        queries,
        new_kv,
        resid,
        kv_cache,
        out_weight,
        gate_weight.T,
        up_weight.T,
        down_weight,
    )


def solution(mesh):
    return jax.shard_map(
        body,
        mesh=mesh,
        in_specs=(
            P("grp", "tp"),
            P(None, "grp", "tp"),
            P(None, "grp", "ffn", "tp"),
            P("grp"),
            P("grp"),
            P("grp", "ffn"),
            P("tp", "ffn"),
            P("ffn"),
            P("ffn", ("grp", "tp")),
            P("ffn", ("grp", "tp")),
            P(("grp", "tp"), "ffn"),
        ),
        out_specs=P(("grp", "tp"), "ffn"),
        check_vma=False,
    )
```

time: 141 us -> 118 us (0.84); the launches traced: 139 us -> 118 us
  local copies, waits for them, and re-layouts: 13.1 us -> 1.42 us
  Pallas kernels: 125 us -> 115 us
    unnamed x13 -> x1, local copies, waits for them, and re-layouts: 11.8 us -> 1.42 us
    pallas_call x2 -> x1, Pallas kernels: 125 us -> 115 us  [layer_call(): pl.pallas_call(layer_kernel, out_shape=jax.ShapeDtypeStruct((ROWS_OUT, WI...]
where the time goes in v2:
time: 118 us
  Pallas kernels  115 us (97%)
  local copies, waits for them, and re-layouts  1.42 us (1%)
  between operations  1.3 us (1%)
    pallas_call x1, Pallas kernels, layer_call(): pl.pallas_call(layer_kernel, out_shape=jax.ShapeDtypeStruct((ROWS_OUT, WI...  115 us

profile of v2, /device:TPU:2, one launch (start us, length us, event | category | flops | bytes accessed | tf_op | source)
XLA Modules:
  0.0 118.1 jit_solution(14783929702389694971)
XLA Ops:
  1.3 115.4 %layer.1 = bf16[24,1024]{1,0:T(8,128)(2,1)} custom-call(s32[1]{0:T(128)S(6)} %copy.13.length_ref, s32[1]{0:T(128)S(6)} %copy.14.prefix_ref, bf16[1024]{0:T(1024)(128)(2,1)} %gain_ref.1, bf16[96,2048]{1,0:T(8,128)(2,1)} %q_hbm.1, bf16[2,96,256]{2,1,0:T(8,128)(2,1)} %new_hbm.1, bf16[96,1024]{1,0:T(8,128)(2,1)} %resid_hbm.1, ...), custom_call_target="tpu_custom_call" | custom-call | tf_op jit(solution)/shard_map/layer/pallas_call | solution.py:513
  116.7 1.4 %copy.15 = bf16[24,1024]{1,0:T(8,128)(2,1)} copy(bf16[24,1024]{1,0:T(8,128)(2,1)} %layer.1) | data formatting | bytes 98304

commit v3 on v2

--- a/solution.py
+++ b/solution.py
@@ -70,6 +70,11 @@
         self.started = []
 
     def start(self, src, dst, device):
+        copy = self.make(src, dst, device)
+        copy.start()
+        return copy
+
+    def make(self, src, dst, device):
         k = len(self.started)
         copy = pltpu.make_async_remote_copy(
             src_ref=src,
@@ -79,7 +84,6 @@
             device_id=device,
             device_id_type=MESH,
         )
-        copy.start()
         self.started.append(copy)
         return copy
 
@@ -131,7 +135,7 @@
     o_out, st_out, o_in, st_in, att, part_f, part_b, part_in, h_ref,
     xs, own_h, sq_out, sq_in,
     send_core, recv_core, keep, stage, recv_one, recv_two, hid,
-    pieces, from_y, summed, za, zb, done, last,
+    pieces, from_y, summed, near, relay, halves, far, done, last,
     local_sems, send_sems, recv_sems,
 ):
     me = Place()
@@ -152,7 +156,7 @@
     friends = [me.ffn((f + d) % 8) for d in range(1, 8)]
     friends += [me.tp((t + d) % 4) for d in range(1, 4)]
     friends += [me.at_y_step(d) for d in range(1, 4)]
-    friends += [me.at_z(1), me.at_z(-1)]
+    friends += [me.at_z(step) for step in (1, -1, 2, -2)]
     greet(friends)
 
     length, prefix = length_ref[0], prefix_ref[0]
@@ -172,8 +176,7 @@
     load_u = load(7, up_hbm, uw)
     load_d = load(8, down_hbm, dw)
 
-    def attend(step, carry):
-        half, h = step // 2, step % 2
+    def attend(half, h):
         cols = pl.ds(pl.multiple_of(h * DH, DH), DH)
         keys, values = kv[0, :, cols], kv[1, :, cols]
         new_keys, new_values = new_ref[0, :, cols], new_ref[1, :, cols]
@@ -204,17 +207,23 @@
             o_out[half * 4 + i, h] = out[rows]
             square = jnp.concatenate([stats[rows], jnp.zeros((32, 128), F32)], axis=0)
             st_out[half * 4 + i, h] = jnp.transpose(square)[:8]
-        return carry
-
-    lax.fori_loop(0, 4, attend, 0)
-
-    greeted(friends)
-    waits = []
-    for d in range(1, 8):
+
+    exchange = []
+    for d in (2, 6, 3, 5, 4, 7, 1):
         to = (f + d) % 8
-        waits.append(links.start(st_out.at[to], st_in.at[d], me.ffn(to)))
-        waits.append(links.start(o_out.at[to], o_in.at[d], me.ffn(to)))
-    arrived(*waits)
+        exchange.append((to, links.make(st_out.at[to], st_in.at[d], me.ffn(to))))
+        exchange.append((to, links.make(o_out.at[to], o_in.at[d], me.ffn(to))))
+    for half in range(2):
+
+        @pl.loop(0, 2)
+        def _(h):
+            attend(half, h)
+
+        if half == 0:
+            greeted(friends)
+        for to, copy in exchange:
+            pl.when(to // 4 == half)(copy.start)
+    arrived(*[copy for to, copy in exchange])
     for h in range(2):
         stats = [st_out[f, h]] + [st_in[d, h] for d in range(1, 8)]
         tops = [s[0:1] for s in stats]
@@ -254,55 +263,59 @@
     for d in range(3):
         h1 += part_in[d].astype(F32)
     h1 = h1.astype(BF16)
-    h_ref[0, z, y] = h1[:, :128]
-    h_ref[1, z, y] = h1[:, 128:]
+    h_ref[z, y] = h1
 
     def pass_on(ref, device):
         return links.start(ref, ref, device)
 
-    def ring(p, row, seen):
-        right = pass_on(h_ref.at[p, z, row], me.at_z(1))
-        left = pass_on(h_ref.at[p, z, row], me.at_z(-1))
-        yield
-        for s in (1, 2, 3):
-            rows = (pl.ds(0, SPAN), pl.ds(0, SPAN)) if s < 3 else (pl.ds(0, 48), pl.ds(48, 48))
-            at = (z - s + 8) % 8
-            arrived(right)
-            right = pass_on(h_ref.at[p, at, row, rows[0]], me.at_z(1))
-            seen(at)
-            at = (z + s) % 8
-            arrived(left)
-            left = pass_on(h_ref.at[p, at, row, rows[1]], me.at_z(-1))
-            seen(at)
-            yield
-        arrived(right, left)
+    low, high = pl.ds(0, 48), pl.ds(48, 48)
+
+    def along_z(row, seen):
+        mine = h_ref.at[z, row]
+        right2, left2 = pass_on(mine, me.at_z(2)), pass_on(mine, me.at_z(-2))
+        right1, left1 = pass_on(mine, me.at_z(1)), pass_on(mine, me.at_z(-1))
+        seen(z)
+        yield
+        at = (z + 6) % 8
+        arrived(right2)
+        right3 = pass_on(h_ref.at[at, row], me.at_z(1))
+        right4 = pass_on(h_ref.at[at, row, low], me.at_z(2))
+        far = (z + 2) % 8
+        arrived(left2)
+        left3 = pass_on(h_ref.at[far, row], me.at_z(-1))
+        left4 = pass_on(h_ref.at[far, row, high], me.at_z(-2))
+        arrived(right1)
+        seen((z + 7) % 8)
+        arrived(left1)
+        seen((z + 1) % 8)
+        seen(at)
+        seen(far)
+        yield
+        arrived(right4, left4)
         seen((z + 4) % 8)
-
-    def from_peer(d):
-        copy = pass_on(h_ref.at[0, z, y], me.at_y_step(d))
+        arrived(right3)
+        seen((z + 5) % 8)
+        arrived(left3)
+        seen((z + 3) % 8)
+
+    def own_rows():
+        waits = []
+
+        def seen(at):
+            for d in (1, 3):
+                waits.append(pass_on(h_ref.at[at, y], me.at_y_step(d)))
+
+        yield from along_z(y, seen)
+        yield
+        arrived(*waits)
+
+    def opposite_rows():
+        copy = pass_on(h_ref.at[z, y], me.at_y_step(2))
         yield
         arrived(copy)
-        yield from ring(0, (y + 4 - d) % 4, lambda at: None)
-
-    def own_then_peers():
-        waits = []
-
-        def seen(at):
-            for d in (1, 2, 3):
-                waits.append(pass_on(h_ref.at[1, at, y], me.at_y_step(d)))
-
-        seen(z)
-        yield from ring(1, y, seen)
-        yield
-        arrived(*waits)
-
-    in_turn(
-        ring(0, y, lambda at: None),
-        from_peer(1),
-        from_peer(3),
-        from_peer(2),
-        own_then_peers(),
-    )
+        yield from along_z((y + 2) % 4, lambda at: None)
+
+    in_turn(opposite_rows(), own_rows())
 
     gain = gain_ref[...].astype(F32).reshape(1, WIDTH)
     lane = lax.broadcasted_iota(jnp.int32, (SPAN, 128), 1)
@@ -310,7 +323,7 @@
 
     def rows_of(side, row):
         return jnp.concatenate(
-            [h_ref[p, side * 4 + k, row] for k in range(4) for p in range(2)], axis=1
+            [h_ref[side * 4 + k, row] for k in range(4)], axis=1
         ).astype(F32)
 
     for g in range(8):
@@ -410,92 +423,75 @@
             for k in range(4):
                 base = i * SPAN + k * ROWS_OUT
                 piece = out[base : base + ROWS_OUT].astype(BF16)
-                for j in range(4):
-                    pieces[j // 2, side * 4 + k, i, j % 2] = piece[:, j * 256 : (j + 1) * 256]
+                for j in range(2):
+                    pieces[side * 4 + k, i, j] = piece[:, j * 512 : (j + 1) * 512]
 
     lower(c)
     arrived(*core_waits)
     lower(1 - c)
 
-    def z_stage(src, got):
-        far = (z + 4) % 8
-        right = links.start(src(far).at[0], got.at[0, 0, 0], me.at_z(1))
-        left = links.start(src(far).at[1], got.at[1, 0, 1], me.at_z(-1))
-        yield
-        for s in (1, 2, 3):
-            for way, at in ((0, (z + 4 - s) % 8), (1, (z + 4 + s) % 8)):
-                ref = src(at)
-                arrived(left if way else right)
-                if s == 1:
-                    ref[way] = plus(ref[way], got[way, 0, way]).astype(BF16)
-                else:
-                    ref[...] = plus(ref[...], got[way, s - 1]).astype(BF16)
-                if way:
-                    left = links.start(ref, got.at[1, s], me.at_z(-1))
-                else:
-                    right = links.start(ref, got.at[0, s], me.at_z(1))
-            yield
-        arrived(right, left)
-
-    def y_first():
+    def along_z_sum(src, near, relay, half, far):
+        copies = []
+        for way, sign in ((0, 1), (1, -1)):
+            copies.append(
+                (
+                    links.start(src(3 * sign), relay.at[way], me.at_z(sign)),
+                    links.start(src(4).at[way], half.at[way], me.at_z(2 * sign)),
+                )
+            )
+        close = [
+            links.start(src(sign), near.at[way], me.at_z(sign))
+            for way, sign in ((0, 1), (1, -1))
+        ]
+        yield
+        ends = []
+        for way, sign in ((0, 1), (1, -1)):
+            ref = src(2 * sign)
+            arrived(*copies[way])
+            ref[1 - way] = plus(ref[1 - way], relay[way, 1 - way]).astype(BF16)
+            ref[way] = plus(ref[way], relay[way, way], half[way]).astype(BF16)
+            ends.append(links.start(ref, far.at[way], me.at_z(2 * sign)))
+        yield
+        src(0)
+        arrived(*close, *ends)
+
+    def own_sum():
         waits = {}
-        for s in (4, 3, 5, 2, 6, 1, 7, 0):
+        for s in (3, 5, 4, 1, 7, 2, 6, 0):
             at = (z + s) % 8
             waits[s] = [
                 links.start(
-                    pieces.at[0, at, (y + d) % 4], from_y.at[d - 1, at], me.at_y_step(d)
+                    pieces.at[at, (y + d) % 4], from_y.at[d // 2, at], me.at_y_step(d)
                 )
-                for d in (1, 3, 2)
+                for d in (1, 3)
             ]
         yield
-        ready = set()
-
-        def src(at_step):
-            at = (z + at_step) % 8
-            if at_step not in ready:
-                arrived(*waits[at_step])
-                summed[at] = plus(
-                    pieces[0, at, y], from_y[0, at], from_y[1, at], from_y[2, at]
-                ).astype(BF16)
-                ready.add(at_step)
+
+        def src(step):
+            at = (z + step + 8) % 8
+            if step % 8 in waits:
+                arrived(*waits.pop(step % 8))
+                summed[at] = plus(pieces[at, y], from_y[0, at], from_y[1, at]).astype(BF16)
             return summed.at[at]
 
-        far = src(4)
-        right = links.start(far.at[0], za.at[0, 0, 0], me.at_z(1))
-        left = links.start(far.at[1], za.at[1, 0, 1], me.at_z(-1))
-        src(3)
-        src(5)
-        yield
-        for s in (1, 2, 3):
-            for way, step in ((0, 4 - s), (1, 4 + s)):
-                ref = src(step)
-                arrived(left if way else right)
-                if s == 1:
-                    ref[way] = plus(ref[way], za[way, 0, way]).astype(BF16)
-                else:
-                    ref[...] = plus(ref[...], za[way, s - 1]).astype(BF16)
-                if way:
-                    left = links.start(ref, za.at[1, s], me.at_z(-1))
-                else:
-                    right = links.start(ref, za.at[0, s], me.at_z(1))
-            yield
-        src(0)
-        arrived(right, left)
-
-    def z_first(d):
-        row = (y + d) % 4
-        got = zb.at[d]
-        yield from z_stage(lambda at: pieces.at[1, at, row], got)
-        if d:
-            done[d - 1] = plus(pieces[1, z, row], got[0, 3], got[1, 3]).astype(BF16)
-            copy = links.start(done.at[d - 1], last.at[d - 1], me.at_y_step(d))
-            yield
-            arrived(copy)
-
-    in_turn(y_first(), z_first(2), z_first(1), z_first(3), z_first(0))
-    left = plus(summed[z], za[0, 3], za[1, 3])
-    right = plus(pieces[1, z, y], zb[0, 0, 3], zb[0, 1, 3], last[0], last[1], last[2])
-    down = jnp.concatenate([left[0], left[1], right[0], right[1]], axis=1)
+        yield from along_z_sum(src, near.at[0], relay.at[0], halves.at[0], far.at[0])
+
+    def opposite_sum():
+        row = (y + 2) % 4
+        yield from along_z_sum(
+            lambda step: pieces.at[(z + step + 8) % 8, row],
+            near.at[1], relay.at[1], halves.at[1], far.at[1],
+        )
+        done[...] = plus(
+            pieces[z, row], near[1, 0], near[1, 1], far[1, 0], far[1, 1]
+        ).astype(BF16)
+        copy = links.start(done, last, me.at_y_step(2))
+        yield
+        arrived(copy)
+
+    in_turn(opposite_sum(), own_sum())
+    total = plus(summed[z], near[0, 0], near[0, 1], far[0, 0], far[0, 1], last[...])
+    down = jnp.concatenate([total[0], total[1]], axis=1)
     start = pl.multiple_of(t * ROWS_OUT, 8)
     out = own_h[pl.ds(start, ROWS_OUT), :] + down
     live = start + lax.broadcasted_iota(jnp.int32, (ROWS_OUT, WIDTH), 0) < length
@@ -507,8 +503,8 @@
     vmem = pl.BlockSpec(memory_space=pltpu.VMEM)
     smem = pl.BlockSpec(memory_space=pltpu.SMEM)
     hbm = pl.BlockSpec(memory_space=pl.ANY)
-    copies = 14 + 7 + 3 + 40 + 3 + 24 + 4 + 7 + 6 + 14 + 24 + 8 + 32 + 3
-    piece = (2, ROWS_OUT, 256)
+    copies = 14 + 7 + 3 + 33 + 4 + 7 + 6 + 14 + 33
+    piece = (2, ROWS_OUT, 512)
     block = (4, 2, 48, BOTH)
     return pl.pallas_call(
         layer_kernel,
@@ -533,7 +529,7 @@
             pltpu.VMEM((4, SPAN, 256), F32),
             pltpu.VMEM((4, SPAN, 256), BF16),
             pltpu.VMEM((3, SPAN, 256), BF16),
-            pltpu.VMEM((2, 8, 4, SPAN, 128), BF16),
+            pltpu.VMEM((8, 4, SPAN, 256), BF16),
             pltpu.VMEM((2, 4, SPAN, WIDTH), BF16),
             pltpu.VMEM((SPAN, WIDTH), F32),
             pltpu.VMEM((8, 8, 128), F32),
@@ -545,13 +541,15 @@
             pltpu.VMEM((2, 2, 48, BOTH), BF16),
             pltpu.VMEM((2, 48, BOTH), BF16),
             pltpu.VMEM((2, 4, 2, 48, WIDTH), BF16),
-            pltpu.VMEM((2, 8, 4) + piece, BF16),
-            pltpu.VMEM((3, 8) + piece, BF16),
+            pltpu.VMEM((8, 4) + piece, BF16),
+            pltpu.VMEM((2, 8) + piece, BF16),
             pltpu.VMEM((8,) + piece, BF16),
-            pltpu.VMEM((2, 4) + piece, BF16),
-            pltpu.VMEM((4, 2, 4) + piece, BF16),
-            pltpu.VMEM((3,) + piece, BF16),
-            pltpu.VMEM((3,) + piece, BF16),
+            pltpu.VMEM((2, 2) + piece, BF16),
+            pltpu.VMEM((2, 2) + piece, BF16),
+            pltpu.VMEM((2, 2, ROWS_OUT, 512), BF16),
+            pltpu.VMEM((2, 2) + piece, BF16),
+            pltpu.VMEM(piece, BF16),
+            pltpu.VMEM(piece, BF16),
             pltpu.SemaphoreType.DMA((9,)),
             pltpu.SemaphoreType.DMA((copies,)),
             pltpu.SemaphoreType.DMA((copies,)),

time: 118 us -> 111 us (0.941)
  Pallas kernels: 115 us -> 108 us
    pallas_call x1, Pallas kernels: 115 us -> 108 us  [layer_call(): pl.pallas_call(layer_kernel, out_shape=jax.ShapeDtypeStruct((ROWS_OUT, WI...]
where the time goes in v3:
time: 111 us
  Pallas kernels  108 us (97%)
  local copies, waits for them, and re-layouts  1.42 us (1%)
  between operations  1.31 us (1%)
    pallas_call x1, Pallas kernels, layer_call(): pl.pallas_call(layer_kernel, out_shape=jax.ShapeDtypeStruct((ROWS_OUT, WI...  108 us

profile of v3, /device:TPU:2, one launch (start us, length us, event | category | flops | bytes accessed | tf_op | source)
XLA Modules:
  0.0 110.6 jit_solution(15520628260633965478)
XLA Ops:
  1.3 107.9 %layer.1 = bf16[24,1024]{1,0:T(8,128)(2,1)} custom-call(s32[1]{0:T(128)S(6)} %copy.13.length_ref, s32[1]{0:T(128)S(6)} %copy.14.prefix_ref, bf16[1024]{0:T(1024)(128)(2,1)} %gain_ref.1, bf16[96,2048]{1,0:T(8,128)(2,1)} %q_hbm.1, bf16[2,96,256]{2,1,0:T(8,128)(2,1)} %new_hbm.1, bf16[96,1024]{1,0:T(8,128)(2,1)} %resid_hbm.1, ...), custom_call_target="tpu_custom_call" | custom-call | tf_op jit(solution)/shard_map/layer/pallas_call | solution.py:509
  109.2 1.4 %copy.15 = bf16[24,1024]{1,0:T(8,128)(2,1)} copy(bf16[24,1024]{1,0:T(8,128)(2,1)} %layer.1) | data formatting | bytes 98304

commit v4 on v3

--- a/solution.py
+++ b/solution.py
@@ -16,6 +16,7 @@
 DH = 128
 SPAN = 96
 ROWS_OUT = 24
+QUERIES = 2
 MAIN = 896
 REST = 28
 BOTH = 1920
@@ -166,8 +167,8 @@
     key = lax.broadcasted_iota(jnp.int32, (SPAN, SPAN), 1)
     limit = jnp.where(f == 0, length, 0)
     new_bias = jnp.where((key <= slot) & (key < limit), 0.0, NEG).astype(F32)
-    new_bias = jnp.concatenate([new_bias] * 4, axis=0)
-    lane = lax.broadcasted_iota(jnp.int32, (4 * SPAN, 128), 1)
+    new_bias = jnp.concatenate([new_bias] * QUERIES, axis=0)
+    lane = lax.broadcasted_iota(jnp.int32, (QUERIES * SPAN, 128), 1)
     for copy in first:
         copy.wait()
     load_wo = load(4, wo_hbm, wo)
@@ -180,33 +181,34 @@
         cols = pl.ds(pl.multiple_of(h * DH, DH), DH)
         keys, values = kv[0, :, cols], kv[1, :, cols]
         new_keys, new_values = new_ref[0, :, cols], new_ref[1, :, cols]
-        q = jnp.concatenate(
-            [
-                q_ref[:, pl.ds(pl.multiple_of((h * 8 + half * 4 + i) * DH, DH), DH)]
-                for i in range(4)
-            ],
-            axis=0,
-        )
-        s = lax.dot_general(q, keys, NT, preferred_element_type=F32) + bias
-        s_new = lax.dot_general(q, new_keys, NT, preferred_element_type=F32) + new_bias
-        top = jnp.maximum(
-            jnp.max(s, axis=1, keepdims=True), jnp.max(s_new, axis=1, keepdims=True)
-        )
-        p = jnp.exp2((s - top) * SCALE).astype(BF16)
-        p_new = jnp.exp2((s_new - top) * SCALE).astype(BF16)
         wide = jnp.concatenate([values, jnp.ones((KEYS, DH), BF16)], axis=1)
         wide_new = jnp.concatenate([new_values, jnp.ones((SPAN, DH), BF16)], axis=1)
-        acc = jnp.dot(p, wide, preferred_element_type=F32) + jnp.dot(
-            p_new, wide_new, preferred_element_type=F32
-        )
-        total = acc[:, DH:]
-        out = (acc[:, :DH] / total).astype(BF16)
-        stats = jnp.where(lane == 0, top, jnp.where(lane == 1, total, 0.0))
-        for i in range(4):
-            rows = slice(i * SPAN, (i + 1) * SPAN)
-            o_out[half * 4 + i, h] = out[rows]
-            square = jnp.concatenate([stats[rows], jnp.zeros((32, 128), F32)], axis=0)
-            st_out[half * 4 + i, h] = jnp.transpose(square)[:8]
+        for first_q in range(half * 4, half * 4 + 4, QUERIES):
+            q = jnp.concatenate(
+                [
+                    q_ref[:, pl.ds(pl.multiple_of((h * 8 + first_q + i) * DH, DH), DH)]
+                    for i in range(QUERIES)
+                ],
+                axis=0,
+            )
+            s = lax.dot_general(q, keys, NT, preferred_element_type=F32) + bias
+            s_new = lax.dot_general(q, new_keys, NT, preferred_element_type=F32) + new_bias
+            top = jnp.maximum(
+                jnp.max(s, axis=1, keepdims=True), jnp.max(s_new, axis=1, keepdims=True)
+            )
+            p = jnp.exp2((s - top) * SCALE).astype(BF16)
+            p_new = jnp.exp2((s_new - top) * SCALE).astype(BF16)
+            acc = jnp.dot(p, wide, preferred_element_type=F32) + jnp.dot(
+                p_new, wide_new, preferred_element_type=F32
+            )
+            total = acc[:, DH:]
+            out = (acc[:, :DH] / total).astype(BF16)
+            stats = jnp.where(lane == 0, top, jnp.where(lane == 1, total, 0.0))
+            for i in range(QUERIES):
+                rows = slice(i * SPAN, (i + 1) * SPAN)
+                o_out[first_q + i, h] = out[rows]
+                square = jnp.concatenate([stats[rows], jnp.zeros((32, 128), F32)], axis=0)
+                st_out[first_q + i, h] = jnp.transpose(square)[:8]
 
     exchange = []
     for d in (2, 6, 3, 5, 4, 7, 1):
@@ -238,7 +240,13 @@
         for d in range(1, 8):
             mine += o_in[d, h].astype(F32) * shares[:, d : d + 1]
         att[f, h] = mine.astype(BF16)
-    waits = [links.start(att.at[f], att.at[f], me.ffn((f + d) % 8)) for d in range(1, 8)]
+    def pass_on(ref, device):
+        return links.start(ref, ref, device)
+
+    core_waits = [pass_on(att.at[f], me.core())]
+    x_waits = [
+        (pass_on(att.at[f], me.at_x((x + d) % 4)), (x + 4 - d) % 4) for d in (2, 1, 3)
+    ]
 
     load_wo.wait()
     load_r.wait()
@@ -247,7 +255,10 @@
     rw[...] = jnp.zeros((128, WIDTH), BF16)
     rw[0:REST] = gw[MAIN:HID]
     rw[64 : 64 + REST] = uw[MAIN:HID]
-    arrived(*waits)
+    for copy, source in (x_waits[1], x_waits[2], x_waits[0]):
+        arrived(copy)
+        core_waits.append(pass_on(att.at[source * 2 + c], me.core()))
+    arrived(*core_waits)
     attn = jnp.concatenate([att[q, h] for h in range(2) for q in range(8)], axis=1)
     part = jnp.dot(attn, wo[...], preferred_element_type=F32)
     for j in range(4):
@@ -265,10 +276,24 @@
     h1 = h1.astype(BF16)
     h_ref[z, y] = h1
 
-    def pass_on(ref, device):
-        return links.start(ref, ref, device)
-
     low, high = pl.ds(0, 48), pl.ds(48, 48)
+
+    gain = gain_ref[...].astype(F32).reshape(1, WIDTH)
+    lane = lax.broadcasted_iota(jnp.int32, (SPAN, 128), 1)
+    squares = [jnp.zeros((SPAN, 128), F32)]
+
+    def rows_of(side, row):
+        return jnp.concatenate(
+            [h_ref[side * 4 + k, row] for k in range(4)], axis=1
+        ).astype(F32)
+
+    def prepare(row):
+        for side in range(2):
+            rows = rows_of(side, row)
+            squares[0] = jnp.where(
+                lane == row * 2 + side, jnp.sum(rows * rows, axis=1, keepdims=True), squares[0]
+            )
+            xs[side, row] = (rows * gain).astype(BF16)
 
     def along_z(row, seen):
         mine = h_ref.at[z, row]
@@ -299,76 +324,89 @@
         seen((z + 3) % 8)
 
     def own_rows():
-        waits = []
+        waits = {1: [], 3: []}
 
         def seen(at):
             for d in (1, 3):
-                waits.append(pass_on(h_ref.at[at, y], me.at_y_step(d)))
+                waits[d].append(pass_on(h_ref.at[at, y], me.at_y_step(d)))
 
         yield from along_z(y, seen)
-        yield
-        arrived(*waits)
+        prepare(y)
+        yield
+        arrived(*waits[1])
+        prepare((y + 3) % 4)
+        arrived(*waits[3])
+        prepare((y + 1) % 4)
 
     def opposite_rows():
         copy = pass_on(h_ref.at[z, y], me.at_y_step(2))
         yield
         arrived(copy)
         yield from along_z((y + 2) % 4, lambda at: None)
+        prepare((y + 2) % 4)
 
     in_turn(opposite_rows(), own_rows())
 
-    gain = gain_ref[...].astype(F32).reshape(1, WIDTH)
-    lane = lax.broadcasted_iota(jnp.int32, (SPAN, 128), 1)
-    squares = jnp.zeros((SPAN, 128), F32)
-
-    def rows_of(side, row):
-        return jnp.concatenate(
-            [h_ref[side * 4 + k, row] for k in range(4)], axis=1
-        ).astype(F32)
-
-    for g in range(8):
-        rows = rows_of(g % 2, g // 2)
-        squares = jnp.where(lane == g, jnp.sum(rows * rows, axis=1, keepdims=True), squares)
-        xs[g % 2, g // 2] = (rows * gain).astype(BF16)
-
-    def project(side, dst):
+    chunks = (pl.ds(0, 1024), pl.ds(1024, MAIN))
+
+    def project(side, dst, k):
         rows = xs[side].reshape(4 * SPAN, WIDTH)
-        for w, base, size in ((gw, 0, MAIN), (uw, MAIN, MAIN), (rw, 2 * MAIN, 128)):
+        parts = ((gw, 0, MAIN), (rw, MAIN, 128)) if k == 0 else ((uw, 1024, MAIN),)
+        for w, base, size in parts:
             out = lax.dot_general(rows, w[0:size], NT, preferred_element_type=F32)
             dst[:, :, :, base : base + size] = out.astype(dst.dtype).reshape(4, 2, 48, size)
 
-    project(1 - c, send_core)
-    core_waits = [
-        links.start(send_core.at[i], recv_core.at[i], me.core()) for i in range(4)
-    ]
-    turned = jnp.transpose(jnp.concatenate([squares, jnp.zeros((32, 128), F32)], axis=0))
+    def to_core(k):
+        project(1 - c, send_core, k)
+        at = (slice(None), slice(None), slice(None), chunks[k])
+        return links.start(send_core.at[at], recv_core.at[at], me.core())
+
+    def joined(i, half, cols):
+        return keep[i, half, :, cols] + recv_core[i, half, :, cols].astype(F32)
+
+    def push(k, half, slot, i, device):
+        cols = chunks[k]
+        stage[i, half, :, cols] = joined(i, half, cols).astype(BF16)
+        return links.start(
+            stage.at[i, half, :, cols], recv_one.at[half, slot, :, cols], device
+        )
+
+    def first_step(k):
+        return (
+            push(k, 0, 1, 3 - me.xa, me.at_x(me.xa)),
+            push(k, 1, 1, flip(me.xb), me.at_x(me.xb)),
+            push(k, 0, 0, me.xa, me.at_x(me.xa)),
+            push(k, 1, 0, me.xb, me.at_x(me.xb)),
+        )
+
+    def second_step(k, far, half, i, device):
+        cols = chunks[k]
+        arrived(far)
+        stage[i, half, :, cols] = plus(
+            joined(i, half, cols), recv_one[half, 1, :, cols]
+        ).astype(BF16)
+        return links.start(stage.at[i, half, :, cols], recv_two.at[half, :, cols], device)
+
+    core_0 = to_core(0)
+    project(c, keep, 0)
+    core_1 = to_core(1)
+    arrived(core_0)
+    step_0 = first_step(0)
+    project(c, keep, 1)
+    arrived(core_1)
+    step_1 = first_step(1)
+    turned = jnp.transpose(jnp.concatenate([squares[0], jnp.zeros((32, 128), F32)], axis=0))
     for g in range(8):
         sq_out[g] = jnp.broadcast_to(turned[g : g + 1], (8, 128))
     sq_waits = []
     for d in range(1, 8):
         to = (f + d) % 8
         sq_waits.append(links.start(sq_out.at[to], sq_in.at[d - 1], me.ffn(to)))
-    project(c, keep)
-    arrived(*core_waits)
-
-    def joined(i, half):
-        return keep[i, half] + recv_core[i, half].astype(F32)
-
-    def push(half, slot, i, device):
-        stage[i, half] = joined(i, half).astype(BF16)
-        return links.start(stage.at[i, half], recv_one.at[half, slot], device)
-
-    far_a = push(0, 1, 3 - me.xa, me.at_x(me.xa))
-    far_b = push(1, 1, flip(me.xb), me.at_x(me.xb))
-    near_a = push(0, 0, me.xa, me.at_x(me.xa))
-    near_b = push(1, 0, me.xb, me.at_x(me.xb))
     own_h[...] = rows_of(me.zh, y)
-    arrived(far_a)
-    stage[me.xb, 0] = (joined(me.xb, 0) + recv_one[0, 1].astype(F32)).astype(BF16)
-    two_a = links.start(stage.at[me.xb, 0], recv_two.at[0], me.at_x(me.xb))
-    arrived(far_b)
-    stage[me.xa, 1] = (joined(me.xa, 1) + recv_one[1, 1].astype(F32)).astype(BF16)
-    two_b = links.start(stage.at[me.xa, 1], recv_two.at[1], me.at_x(me.xa))
+    two_a, two_b = [], []
+    for k, step in ((0, step_0), (1, step_1)):
+        two_a.append(second_step(k, step[0], 0, me.xb, me.at_x(me.xb)))
+        two_b.append(second_step(k, step[1], 1, me.xa, me.at_x(me.xa)))
 
     arrived(*sq_waits)
     total = sq_out[f]
@@ -381,21 +419,21 @@
         return v / (1.0 + jnp.exp(-v))
 
     def activate(half):
-        both = plus(joined(x, half), recv_one[half, 0], recv_two[half])
+        both = plus(joined(x, half, slice(None)), recv_one[half, 0], recv_two[half])
         both = both * rs[half * 48 : (half + 1) * 48]
-        rest = both[:, 2 * MAIN :]
-        hid[c, x, half, :, 0:MAIN] = (silu(both[:, :MAIN]) * both[:, MAIN : 2 * MAIN]).astype(BF16)
+        rest = both[:, MAIN:1024]
+        hid[c, x, half, :, 0:MAIN] = (silu(both[:, :MAIN]) * both[:, 1024:]).astype(BF16)
         hid[c, x, half, :, MAIN:] = (silu(rest) * pltpu.roll(rest, 64, 1)).astype(BF16)
 
     def share(half, i, device):
         return pass_on(hid.at[c, i, half], device)
 
-    arrived(near_a, two_a)
+    arrived(step_0[2], step_1[2], *two_a)
     activate(0)
     a0 = share(0, x, me.at_x(me.xa))
     b0 = share(0, x, me.at_x(me.xb))
     core_waits = [share(0, x, me.core())]
-    arrived(near_b, two_b)
+    arrived(step_0[3], step_1[3], *two_b)
     activate(1)
     b1 = share(1, x, me.at_x(me.xb))
     a1 = share(1, x, me.at_x(me.xa))
@@ -503,7 +541,7 @@
     vmem = pl.BlockSpec(memory_space=pltpu.VMEM)
     smem = pl.BlockSpec(memory_space=pltpu.SMEM)
     hbm = pl.BlockSpec(memory_space=pl.ANY)
-    copies = 14 + 7 + 3 + 33 + 4 + 7 + 6 + 14 + 33
+    copies = 14 + 7 + 3 + 33 + 2 + 7 + 12 + 14 + 33
     piece = (2, ROWS_OUT, 512)
     block = (4, 2, 48, BOTH)
     return pl.pallas_call(

time: 111 us -> 105 us (0.946)
  Pallas kernels: 108 us -> 102 us
    pallas_call x1, Pallas kernels: 108 us -> 102 us  [layer_call(): pl.pallas_call(layer_kernel, out_shape=jax.ShapeDtypeStruct((ROWS_OUT, WI...]
where the time goes in v4:
time: 105 us
  Pallas kernels  102 us (97%)
  local copies, waits for them, and re-layouts  1.42 us (1%)
  between operations  1.3 us (1%)
    pallas_call x1, Pallas kernels, layer_call(): pl.pallas_call(layer_kernel, out_shape=jax.ShapeDtypeStruct((ROWS_OUT, WI...  102 us

profile of v4, /device:TPU:2, one launch (start us, length us, event | category | flops | bytes accessed | tf_op | source)
XLA Modules:
  0.0 104.7 jit_solution(17010863961035525541)
XLA Ops:
  1.3 102.0 %layer.1 = bf16[24,1024]{1,0:T(8,128)(2,1)} custom-call(s32[1]{0:T(128)S(6)} %copy.13.length_ref, s32[1]{0:T(128)S(6)} %copy.14.prefix_ref, bf16[1024]{0:T(1024)(128)(2,1)} %gain_ref.1, bf16[96,2048]{1,0:T(8,128)(2,1)} %q_hbm.1, bf16[2,96,256]{2,1,0:T(8,128)(2,1)} %new_hbm.1, bf16[96,1024]{1,0:T(8,128)(2,1)} %resid_hbm.1, ...), custom_call_target="tpu_custom_call" | custom-call | tf_op jit(solution)/shard_map/layer/pallas_call | solution.py:547
  103.3 1.4 %copy.15 = bf16[24,1024]{1,0:T(8,128)(2,1)} copy(bf16[24,1024]{1,0:T(8,128)(2,1)} %layer.1) | data formatting | bytes 98304

commit v5 on v4

--- a/solution.py
+++ b/solution.py
@@ -217,8 +217,7 @@
         exchange.append((to, links.make(o_out.at[to], o_in.at[d], me.ffn(to))))
     for half in range(2):
 
-        @pl.loop(0, 2)
-        def _(h):
+        for h in range(2):
             attend(half, h)
 
         if half == 0:

time: 105 us -> 103 us (0.981)
  Pallas kernels: 102 us -> 100 us
    pallas_call x1, Pallas kernels: 102 us -> 100 us  [layer_call(): pl.pallas_call(layer_kernel, out_shape=jax.ShapeDtypeStruct((ROWS_OUT, WI...]
where the time goes in v5:
time: 103 us
  Pallas kernels  100 us (97%)
  local copies, waits for them, and re-layouts  1.42 us (1%)
  between operations  1.3 us (1%)
    pallas_call x1, Pallas kernels, layer_call(): pl.pallas_call(layer_kernel, out_shape=jax.ShapeDtypeStruct((ROWS_OUT, WI...  100 us

profile of v5, /device:TPU:2, one launch (start us, length us, event | category | flops | bytes accessed | tf_op | source)
XLA Modules:
  0.0 102.9 jit_solution(17091190845492238088)
XLA Ops:
  1.3 100.2 %layer.1 = bf16[24,1024]{1,0:T(8,128)(2,1)} custom-call(s32[1]{0:T(128)S(6)} %copy.13.length_ref, s32[1]{0:T(128)S(6)} %copy.14.prefix_ref, bf16[1024]{0:T(1024)(128)(2,1)} %gain_ref.1, bf16[96,2048]{1,0:T(8,128)(2,1)} %q_hbm.1, bf16[2,96,256]{2,1,0:T(8,128)(2,1)} %new_hbm.1, bf16[96,1024]{1,0:T(8,128)(2,1)} %resid_hbm.1, ...), custom_call_target="tpu_custom_call" | custom-call | tf_op jit(solution)/shard_map/layer/pallas_call | solution.py:546
  101.5 1.4 %copy.15 = bf16[24,1024]{1,0:T(8,128)(2,1)} copy(bf16[24,1024]{1,0:T(8,128)(2,1)} %layer.1) | data formatting | bytes 98304

commit v6 on v5

--- a/solution.py
+++ b/solution.py
@@ -177,13 +177,13 @@
     load_u = load(7, up_hbm, uw)
     load_d = load(8, down_hbm, dw)
 
-    def attend(half, h):
+    def attend(phase, h):
         cols = pl.ds(pl.multiple_of(h * DH, DH), DH)
         keys, values = kv[0, :, cols], kv[1, :, cols]
         new_keys, new_values = new_ref[0, :, cols], new_ref[1, :, cols]
         wide = jnp.concatenate([values, jnp.ones((KEYS, DH), BF16)], axis=1)
         wide_new = jnp.concatenate([new_values, jnp.ones((SPAN, DH), BF16)], axis=1)
-        for first_q in range(half * 4, half * 4 + 4, QUERIES):
+        for first_q in range(phase[0], phase[1], QUERIES):
             q = jnp.concatenate(
                 [
                     q_ref[:, pl.ds(pl.multiple_of((h * 8 + first_q + i) * DH, DH), DH)]
@@ -215,15 +215,13 @@
         to = (f + d) % 8
         exchange.append((to, links.make(st_out.at[to], st_in.at[d], me.ffn(to))))
         exchange.append((to, links.make(o_out.at[to], o_in.at[d], me.ffn(to))))
-    for half in range(2):
-
+    for phase in ((0, 4), (4, 6), (6, 8)):
         for h in range(2):
-            attend(half, h)
-
-        if half == 0:
+            attend(phase, h)
+        if phase[0] == 0:
             greeted(friends)
         for to, copy in exchange:
-            pl.when(to // 4 == half)(copy.start)
+            pl.when((to >= phase[0]) & (to < phase[1]))(copy.start)
     arrived(*[copy for to, copy in exchange])
     for h in range(2):
         stats = [st_out[f, h]] + [st_in[d, h] for d in range(1, 8)]

time: 103 us -> 103 us (level)
  no operation moved by 1% of the time
where the time goes in v6:
time: 103 us
  Pallas kernels  99.8 us (97%)
  local copies, waits for them, and re-layouts  1.42 us (1%)
  between operations  1.3 us (1%)
    pallas_call x1, Pallas kernels, layer_call(): pl.pallas_call(layer_kernel, out_shape=jax.ShapeDtypeStruct((ROWS_OUT, WI...  99.8 us

profile of v6, /device:TPU:2, one launch (start us, length us, event | category | flops | bytes accessed | tf_op | source)
XLA Modules:
  0.0 102.6 jit_solution(1485737331124186095)
XLA Ops:
  1.3 99.8 %layer.1 = bf16[24,1024]{1,0:T(8,128)(2,1)} custom-call(s32[1]{0:T(128)S(6)} %copy.13.length_ref, s32[1]{0:T(128)S(6)} %copy.14.prefix_ref, bf16[1024]{0:T(1024)(128)(2,1)} %gain_ref.1, bf16[96,2048]{1,0:T(8,128)(2,1)} %q_hbm.1, bf16[2,96,256]{2,1,0:T(8,128)(2,1)} %new_hbm.1, bf16[96,1024]{1,0:T(8,128)(2,1)} %resid_hbm.1, ...), custom_call_target="tpu_custom_call" | custom-call | tf_op jit(solution)/shard_map/layer/pallas_call | solution.py:544
  101.1 1.4 %copy.15 = bf16[24,1024]{1,0:T(8,128)(2,1)} copy(bf16[24,1024]{1,0:T(8,128)(2,1)} %layer.1) | data formatting | bytes 98304
